TPU v7x, 128 devices: a whole 4x4x4 slice. The times are simulated.
128 devices in a mesh: dp: 32 (over y, z, x_lo), mp: 4 (over x_hi, core).
Axes of the slice: x: 4 (x_hi: 2, x_lo: 2; x = x_hi * 2 + x_lo), y: 4, z: 4, core: 2. Of those that a mesh axis runs over, the one named last changes fastest.
Arguments:
- hidden_in: bfloat16 [16384, 1024], P('dp'), may hold values from -6 to 6
- lengths: int32 [16], replicated, may hold values from 1 to 4, 32 in all
- block_order: int32 [32], replicated, may hold values from 0 to 31, each once
- routes: int32 [16384, 8], P('dp'), may hold values from 0 to 31, all different within a row; in each aligned block of 512 rows (0 to 511, 512 to 1023, ...) at most 160 rows name the same one
- norm_gain_attn: float32 [1024], replicated, may hold values from 0.25 to 1.75
- w_query: bfloat16 [1024, 1024], P(None, 'mp'), may hold values from -0.75 to 0.75
- w_key: bfloat16 [1024, 512], P(None, 'mp'), may hold values from -0.75 to 0.75
- w_value: bfloat16 [1024, 512], P(None, 'mp'), may hold values from -0.1875 to 0.1875
- w_out: bfloat16 [1024, 1024], P('mp'), may hold values from -3 to 3
- norm_gain_moe: float32 [1024], replicated, may hold values from 0.25 to 1.75
- w_router: bfloat16 [1024, 32], replicated, may hold values from -0.09375 to 0.09375
- w_gate: bfloat16 [32, 1024, 512], P('dp', None, 'mp'), may hold values from -0.1875 to 0.1875
- w_up: bfloat16 [32, 1024, 512], P('dp', None, 'mp'), may hold values from -0.1875 to 0.1875
- w_down: bfloat16 [32, 512, 1024], P('dp', 'mp'), may hold values from -3 to 3
- out_grad: bfloat16 [16384, 1024], P('dp'), may hold values from -6 to 6
Outputs:
- out_hidden: bfloat16 [16384, 1024], P('dp', 'mp')
- grad_hidden: float32 [16384, 1024], P('dp', 'mp')
- grad_w_query: float32 [1024, 1024], P('dp', 'mp')
- grad_w_key: float32 [1024, 512], P('dp', 'mp')
- grad_w_value: float32 [1024, 512], P('dp', 'mp')
- grad_w_out: float32 [1024, 1024], P('mp', 'dp')
- grad_gain_attn: float32 [1024], P('dp')
- grad_gain_moe: float32 [1024], P('dp')
- grad_w_router: float32 [1024, 32], P('dp')
- grad_w_gate: float32 [32, 1024, 512], P('dp', None, 'mp')
- grad_w_up: float32 [32, 1024, 512], P('dp', None, 'mp')
- grad_w_down: float32 [32, 512, 1024], P('dp', 'mp')
Inputs may be any that keep to these rules, and one draw needn't show every extreme that they name: lengths count blocks of 512 tokens of the packed sequences; they sum to 32 and the largest is exactly 4. `block_order`: each of 0 to 31 appears once. `routes`: each token names 8 different experts; among the 512 tokens of one index of dp no expert is named by more than 160 tokens, and in some of these aligned blocks one expert is named by exactly 160.
All inputs are finite; a program needn't handle non-finite values.
Results may differ from a plain program's by a relative error of at most 0.034.
Values may be sent and summed in bfloat16 or wider, within the bound.
No kernel may reach another device: no remote copies, remote signals or barrier semaphores. Data moves between devices by JAX's collectives and lax.ppermute only.
A program may use at most 128 MiB of HBM per device.

v0:
```python
import jax
import jax.numpy as jnp
from jax import lax
from jax.sharding import PartitionSpec as P

HEAD_DIM = 64
EXPERTS = 32
BLOCK = 512
MAXLEN = 2048
CAP = 160


epsilon = 1e-06
residual_mult = 0.22
score_mult = 0.015625
rope_base = 10000.0
masked_score = -1e30


def in_one_piece(arrays, axis, dim, along):
    ends, at = ([], 0)
    for a in arrays[:-1]:
        at += a.shape[along]
        ends.append(at)
    both = jnp.concatenate(arrays, axis=along)
    return tuple(jnp.split(lax.all_gather(both, axis, axis=dim, tiled=True), ends, axis=along))


def gathered_total(x, axis):
    parts = lax.all_gather(x, axis).astype(jnp.float32)
    return parts.sum(axis=0)


def turned_gather(arrays, axis, dims):
    turned = [jnp.moveaxis(a, dim, 0) for a, dim in zip(arrays, dims)]
    both = jnp.concatenate([t.reshape(len(t), -1) for t in turned], axis=1)
    result, at, finished = (lax.all_gather(both, axis, axis=0, tiled=True), 0, [])
    for t, dim in zip(turned, dims):
        share = result[:, at : at + t[0].size].reshape(-1, *t.shape[1:])
        finished.append(jnp.moveaxis(share, 0, dim))
        at += t[0].size
    return tuple(finished)


def in_blocks(x, dim, length):
    before, after = (x.shape[:dim], x.shape[dim + 1 :])
    return jnp.moveaxis(x.reshape(*before, length, -1, *after), dim, 0)


def laid_out(parts, dim):
    dims = list(parts.shape[1:])
    dims[dim] *= parts.shape[0]
    return jnp.moveaxis(parts, 0, dim).reshape(dims)


def exchange_both(x, axis, axes, splits, concats):
    sizes = [lax.axis_size(a) for a in axes]
    parts = in_blocks(x, splits[0], sizes[0])
    parts = jnp.moveaxis(in_blocks(parts, splits[1] + 1, sizes[1]), 0, 1)
    inside = parts.shape[2:]
    parts = parts.reshape(-1, *inside)
    parts = lax.all_to_all(parts, axis, split_axis=0, concat_axis=0, tiled=True)
    parts = laid_out(parts.reshape(*sizes, *inside), concats[0] + 1)
    return laid_out(parts, concats[1])


def in_one_piece_2(arrays, axis, dim, along):
    ends, at = ([], 0)
    for a in arrays[:-1]:
        at += a.shape[along]
        ends.append(at)
    both = jnp.concatenate(arrays, axis=along)
    return tuple(
        jnp.split(lax.psum_scatter(both, axis, scatter_dimension=dim, tiled=True), ends, axis=along)
    )


def sent_to_all(x, axis):
    length = lax.axis_size(axis)
    return lax.all_to_all(jnp.broadcast_to(x[None], (length, *x.shape)), axis, 0, 0, tiled=True)


def gathered_copies(x, axis, dim):
    parts = sent_to_all(x, axis)
    return laid_out(parts, dim)


def in_one_piece_3(arrays, axis, dim, along):
    columns = [a.reshape(*a.shape[:along], -1) for a in arrays]
    both = jnp.concatenate(columns, axis=along)
    result, at, finished = (lax.psum_scatter(both, axis, scatter_dimension=dim, tiled=True), 0, [])
    for a, column in zip(arrays, columns):
        share = result[..., at : at + column.shape[along]]
        finished.append(share.reshape(*share.shape[:along], *a.shape[along:]))
        at += column.shape[along]
    return tuple(finished)


def rms_scale(row_values):
    return lax.rsqrt(jnp.mean(row_values * row_values, axis=-1, keepdims=True) + epsilon)


def norm_back(row_values, norm_scale, gain_values, incoming):
    weighted = incoming * gain_values
    inner_mean = jnp.mean(weighted * row_values, axis=-1, keepdims=True)
    return norm_scale * weighted - row_values * (norm_scale * norm_scale * norm_scale) * inner_mean


def rope_tables(positions):
    half_dim = HEAD_DIM // 2
    frequency = rope_base ** (-(jnp.arange(half_dim, dtype=jnp.float32) * 2.0) / HEAD_DIM)
    angles = positions.astype(jnp.float32)[:, None] * frequency[None, :]
    return (jnp.cos(angles), jnp.sin(angles))


def rotate(row_values, cosine, sine_table):
    half_dim = HEAD_DIM // 2
    shaped = row_values.reshape(row_values.shape[0], row_values.shape[1] // HEAD_DIM, HEAD_DIM)
    front_half = shaped[:, :, :half_dim]
    back_half = shaped[:, :, half_dim:]
    cosine_wide = cosine[:, None, :]
    sine_wide = sine_table[:, None, :]
    turned = jnp.concatenate(
        [
            front_half * cosine_wide - back_half * sine_wide,
            back_half * cosine_wide + front_half * sine_wide,
        ],
        axis=-1,
    )
    return turned.reshape(row_values.shape)


def rotate_back(row_values, cosine, sine_table):
    half_dim = HEAD_DIM // 2
    shaped = row_values.reshape(row_values.shape[0], row_values.shape[1] // HEAD_DIM, HEAD_DIM)
    front_half = shaped[:, :, :half_dim]
    back_half = shaped[:, :, half_dim:]
    cosine_wide = cosine[:, None, :]
    sine_wide = sine_table[:, None, :]
    turned = jnp.concatenate(
        [
            front_half * cosine_wide + back_half * sine_wide,
            back_half * cosine_wide - front_half * sine_wide,
        ],
        axis=-1,
    )
    return turned.reshape(row_values.shape)


def block_tables(lengths, block_order):
    block_ids = jnp.arange(block_order.shape[0], dtype=jnp.int32)
    sequence_ids = jnp.arange(lengths.shape[0], dtype=jnp.int32)
    sequence_ends = jnp.cumsum(lengths)
    sequence_starts = sequence_ends - lengths
    sequence_of = jnp.sum((sequence_ends[None, :] <= block_ids[:, None]).astype(jnp.int32), axis=1)
    begins = jnp.sum(
        jnp.where(sequence_of[:, None] == sequence_ids[None, :], sequence_starts[None, :], 0),
        axis=1,
    )
    offsets = block_ids - begins
    inverse = jnp.sum(
        jnp.where(block_order[None, :] == block_ids[:, None], block_ids[None, :], 0), axis=1
    )
    return (offsets, inverse)


def row_contract(left_side, right_side):
    return lax.dot_general(
        left_side, right_side, (((0,), (0,)), ((), ())), preferred_element_type=jnp.float32
    )


def times_transposed(left_side, right_side):
    return lax.dot_general(
        left_side, right_side, (((1,), (1,)), ((), ())), preferred_element_type=jnp.float32
    )


def expert_back(grouped_in, grouped_grad, gate_pre, up_pre, gate_mat, up_mat, down_mat):
    sigmoid_gate = jax.nn.sigmoid(gate_pre)
    silu_gate = jax.nn.silu(gate_pre)
    hidden_units = (silu_gate * up_pre).astype(jnp.bfloat16)
    down_grad = jnp.einsum(
        "secf,secd->efd", hidden_units, grouped_grad, preferred_element_type=jnp.float32
    )
    hidden_grad = jnp.einsum(
        "secd,efd->secf", grouped_grad, down_mat, preferred_element_type=jnp.float32
    )
    gate_pre_grad = (
        hidden_grad * up_pre * sigmoid_gate * (1.0 + gate_pre * (1.0 - sigmoid_gate))
    ).astype(jnp.bfloat16)
    up_pre_grad = (hidden_grad * silu_gate).astype(jnp.bfloat16)
    gate_w_grad = jnp.einsum(
        "secd,secf->edf", grouped_in, gate_pre_grad, preferred_element_type=jnp.float32
    )
    up_w_grad = jnp.einsum(
        "secd,secf->edf", grouped_in, up_pre_grad, preferred_element_type=jnp.float32
    )
    input_part = jnp.einsum(
        "secf,edf->secd", gate_pre_grad, gate_mat, preferred_element_type=jnp.float32
    ) + jnp.einsum("secf,edf->secd", up_pre_grad, up_mat, preferred_element_type=jnp.float32)
    return (gate_w_grad, up_w_grad, down_grad, input_part)


def per_device(
    hidden_in,
    lengths,
    block_order,
    routes,
    norm_gain_attn,
    w_query,
    w_key,
    w_value,
    w_out,
    norm_gain_moe,
    w_router,
    w_gate,
    w_up,
    w_down,
    out_grad,
):
    dp_count = lax.axis_size("dp")
    mp_count = lax.axis_size("mp")
    dp_rank = lax.axis_index("dp")
    mp_rank = lax.axis_index("mp")
    tokens_here = hidden_in.shape[0]
    model_width = hidden_in.shape[1]
    column_share = model_width // mp_count
    column_start = mp_rank * column_share
    blocks_here = tokens_here // BLOCK
    window = MAXLEN // BLOCK
    kv_here = w_key.shape[1] // HEAD_DIM
    head_group = w_query.shape[1] // HEAD_DIM // kv_here
    experts_here = w_gate.shape[0]
    route_width = routes.shape[1]
    capacity = CAP
    offsets, inverse = block_tables(lengths, block_order)
    block_ids = jnp.arange(block_order.shape[0], dtype=jnp.int32)
    my_blocks = lax.dynamic_slice_in_dim(block_order, dp_rank * blocks_here, blocks_here)
    my_offsets = jnp.sum(
        jnp.where(my_blocks[:, None] == block_ids[None, :], offsets[None, :], 0), axis=1
    )
    row_ids = jnp.arange(BLOCK, dtype=jnp.int32)
    positions = (my_offsets[:, None] * BLOCK + row_ids[None, :]).reshape(-1)
    cosine, sine_table = rope_tables(positions)
    later_keys = row_ids[None, :] > row_ids[:, None]
    input_full = hidden_in.astype(jnp.float32)
    scale_one = rms_scale(input_full)
    normed = (input_full * scale_one * norm_gain_attn).astype(jnp.bfloat16)
    query_pre = jnp.dot(normed, w_query, preferred_element_type=jnp.float32)
    key_pre = jnp.dot(normed, w_key, preferred_element_type=jnp.float32)
    value_pre = jnp.dot(normed, w_value, preferred_element_type=jnp.float32)
    queries = rotate(query_pre, cosine, sine_table).astype(jnp.bfloat16)
    key_rows = rotate(key_pre, cosine, sine_table).astype(jnp.bfloat16)
    value_rows = value_pre.astype(jnp.bfloat16)
    keys_all, values_all = in_one_piece((key_rows, value_rows), "dp", 0, 1)

    def key_block(packed_query, key_step):
        packed_key = jnp.maximum(packed_query - key_step, 0)
        source = jnp.sum(jnp.where(block_ids == packed_key, inverse, 0))
        row_start = source * BLOCK
        return (
            lax.dynamic_slice_in_dim(keys_all, row_start, BLOCK, 0),
            lax.dynamic_slice_in_dim(values_all, row_start, BLOCK, 0),
            row_start,
        )

    def block_scores(query_block, key_block_rows, key_step):
        query_heads = query_block.reshape(BLOCK, kv_here, head_group, HEAD_DIM)
        key_heads = key_block_rows.reshape(BLOCK, kv_here, HEAD_DIM)
        raw_scores = (
            jnp.einsum("qhgd,khd->hgqk", query_heads, key_heads, preferred_element_type=jnp.float32)
            * score_mult
        )
        return jnp.where(jnp.logical_and(key_step == 0, later_keys), masked_score, raw_scores)

    local_block = 0
    packed_query = my_blocks[local_block]
    block_reach = my_offsets[local_block]
    query_block = queries

    def max_step(
        key_step,
        max_state,
        packed_query=packed_query,
        block_reach=block_reach,
        query_block=query_block,
    ):

        def max_live(running):
            running_max, running_sum = running
            key_part, value_part, row_start = key_block(packed_query, key_step)
            scores = block_scores(query_block, key_part, key_step)
            new_max = jnp.maximum(running_max, jnp.max(scores, axis=-1))
            new_sum = running_sum * jnp.exp(running_max - new_max) + jnp.sum(
                jnp.exp(scores - new_max[..., None]), axis=-1
            )
            return (new_max, new_sum)

        return lax.cond(key_step <= block_reach, max_live, lambda running: running, max_state)

    start_state = (
        jnp.full((kv_here, head_group, BLOCK), masked_score, jnp.float32),
        jnp.zeros((kv_here, head_group, BLOCK), jnp.float32),
    )
    running_max, running_sum = lax.fori_loop(0, window, max_step, start_state)
    block_lse = running_max + jnp.log(running_sum)

    def sum_step(
        key_step,
        accumulated,
        packed_query=packed_query,
        block_reach=block_reach,
        query_block=query_block,
        block_lse=block_lse,
    ):

        def sum_live(running_total):
            key_part, value_part, row_start = key_block(packed_query, key_step)
            prob_block = jnp.exp(
                block_scores(query_block, key_part, key_step) - block_lse[..., None]
            ).astype(jnp.bfloat16)
            value_heads = value_part.reshape(BLOCK, kv_here, HEAD_DIM)
            return running_total + jnp.einsum(
                "hgqk,khd->qhgd", prob_block, value_heads, preferred_element_type=jnp.float32
            )

        return lax.cond(
            key_step <= block_reach, sum_live, lambda running_total: running_total, accumulated
        )

    block_out = lax.fori_loop(
        0, window, sum_step, jnp.zeros((BLOCK, kv_here, head_group, HEAD_DIM), jnp.float32)
    )
    attended_blocks = block_out.reshape(BLOCK, kv_here * head_group * HEAD_DIM)
    lse_blocks = [block_lse]
    attended = attended_blocks.astype(jnp.bfloat16)
    branch_part = jnp.dot(attended, w_out, preferred_element_type=jnp.float32)
    branch = gathered_total(branch_part.astype(jnp.bfloat16), "mp").astype(jnp.float32)
    residual = input_full + residual_mult * branch
    scale_two = rms_scale(residual)
    moe_in = (residual * scale_two * norm_gain_moe).astype(jnp.bfloat16)
    logits = jnp.dot(moe_in, w_router, preferred_element_type=jnp.float32)
    expert_ids = jnp.arange(EXPERTS, dtype=jnp.int32)
    chosen = routes[:, :, None] == expert_ids[None, None, :]
    picked = jnp.sum(jnp.where(chosen, logits[:, None, :], 0.0), axis=2)
    gate_weights = jax.nn.softmax(picked, axis=-1)
    expert_hits = jnp.sum(chosen.astype(jnp.int32), axis=1)
    rank_table = jnp.cumsum(expert_hits, axis=0) - expert_hits
    pair_rank = jnp.sum(jnp.where(chosen, rank_table[:, None, :], 0), axis=2)
    pair_slot = (routes * capacity + pair_rank).reshape(-1)
    token_ids = jnp.arange(tokens_here, dtype=jnp.int32)
    token_fill = jnp.broadcast_to(token_ids[:, None], (tokens_here, route_width)).reshape(-1)
    slot_token = (
        jnp.full((EXPERTS * capacity,), tokens_here, jnp.int32).at[pair_slot].set(token_fill)
    )
    slot_gate = (
        jnp.zeros((EXPERTS * capacity,), jnp.float32).at[pair_slot].set(gate_weights.reshape(-1))
    )
    padded_moe = jnp.concatenate([moe_in, jnp.zeros((1, model_width), jnp.bfloat16)], axis=0)
    padded_grad = jnp.concatenate([out_grad, jnp.zeros((1, model_width), jnp.bfloat16)], axis=0)
    quarter = capacity // mp_count
    slot_begin = mp_rank * quarter
    token_part = lax.dynamic_slice_in_dim(
        slot_token.reshape(EXPERTS, capacity), slot_begin, quarter, 1
    ).reshape(-1)
    gate_part_slots = lax.dynamic_slice_in_dim(
        slot_gate.reshape(EXPERTS, capacity), slot_begin, quarter, 1
    ).reshape(-1)
    full_gate, full_up, full_down = turned_gather((w_gate, w_up, w_down), "mp", (2, 2, 1))
    outgoing = jnp.take(padded_moe, token_part, axis=0).reshape(EXPERTS, quarter, model_width)
    arrived = lax.all_to_all(outgoing, "dp", split_axis=0, concat_axis=0, tiled=True)
    held_slots = arrived.shape[1]
    grouped = arrived.reshape(dp_count, experts_here, held_slots, model_width)
    gate_pre = jnp.einsum("secd,edf->secf", grouped, full_gate, preferred_element_type=jnp.float32)
    up_pre = jnp.einsum("secd,edf->secf", grouped, full_up, preferred_element_type=jnp.float32)
    hidden_units = (jax.nn.silu(gate_pre) * up_pre).astype(jnp.bfloat16)
    rows_out = jnp.einsum(
        "secf,efd->secd", hidden_units, full_down, preferred_element_type=jnp.float32
    ).astype(jnp.bfloat16)
    rows_out, expert_in, gate_keep, up_keep = (
        rows_out.reshape(dp_count * experts_here, held_slots, model_width),
        arrived,
        gate_pre.reshape(dp_count * experts_here, held_slots, -1),
        up_pre.reshape(dp_count * experts_here, held_slots, -1),
    )
    returned = exchange_both(rows_out, ("dp", "mp"), ("dp", "mp"), (0, 2), (0, 1))
    slot_factor = (residual_mult * gate_part_slots)[:, None]
    outgoing_grad = (
        (jnp.take(padded_grad, token_part, axis=0).astype(jnp.float32) * slot_factor)
        .astype(jnp.bfloat16)
        .reshape(EXPERTS, quarter, model_width)
    )
    arrived_grad = lax.all_to_all(outgoing_grad, "dp", split_axis=0, concat_axis=0, tiled=True)
    shape_four = (dp_count, experts_here, quarter)
    gate_w_part, up_w_part, down_w_part, input_part = expert_back(
        expert_in.reshape(shape_four + (model_width,)),
        arrived_grad.reshape(shape_four + (model_width,)),
        gate_keep.reshape(shape_four + (gate_keep.shape[2],)),
        up_keep.reshape(shape_four + (up_keep.shape[2],)),
        full_gate,
        full_up,
        full_down,
    )
    grad_w_gate, grad_w_up, grad_w_down = (
        *tuple(
            (
                part.astype(jnp.float32)
                for part in in_one_piece_2(
                    (gate_w_part.astype(jnp.bfloat16), up_w_part.astype(jnp.bfloat16)), "mp", 2, 0
                )
            )
        ),
        lax.psum_scatter(
            down_w_part.astype(jnp.bfloat16), "mp", scatter_dimension=1, tiled=True
        ).astype(jnp.float32),
    )
    input_home = exchange_both(
        input_part.astype(jnp.bfloat16).reshape(dp_count * experts_here, quarter, model_width),
        ("dp", "mp"),
        ("dp", "mp"),
        (0, 2),
        (0, 1),
    )
    picked_rows = (
        jnp.take(returned.reshape(EXPERTS * capacity, column_share), pair_slot, axis=0)
        .reshape(tokens_here, route_width, column_share)
        .astype(jnp.float32)
    )
    mixture = jnp.sum(gate_weights[:, :, None] * picked_rows, axis=1)
    residual_cols = lax.dynamic_slice_in_dim(residual, column_start, column_share, 1)
    out_hidden = (residual_cols + residual_mult * mixture).astype(jnp.bfloat16)
    grad_full = out_grad.astype(jnp.float32)
    grad_own_cols = lax.dynamic_slice_in_dim(grad_full, column_start, column_share, 1)
    gate_part = residual_mult * jnp.sum(grad_own_cols[:, None, :] * picked_rows, axis=2)
    home_rows = jnp.take(
        input_home.reshape(EXPERTS * capacity, column_share), pair_slot, axis=0
    ).reshape(tokens_here, route_width, column_share)
    expert_grad_cols = jnp.sum(home_rows.astype(jnp.float32), axis=1)
    expert_grad, gate_parts = (
        gathered_copies(expert_grad_cols.astype(jnp.bfloat16), "mp", 1).astype(
            expert_grad_cols.dtype
        ),
        gathered_copies(gate_part.astype(jnp.bfloat16), "mp", 1).astype(gate_part.dtype),
    )
    gate_total = jnp.sum(gate_parts.reshape(tokens_here, mp_count, route_width), axis=1)
    select_grad = gate_weights * (
        gate_total - jnp.sum(gate_weights * gate_total, axis=-1, keepdims=True)
    )
    logit_grad = jnp.sum(jnp.where(chosen, select_grad[:, :, None], 0.0), axis=1).astype(
        jnp.bfloat16
    )
    moe_in_grad = expert_grad + times_transposed(logit_grad, w_router)
    router_grad = row_contract(moe_in, logit_grad)
    moe_gain_grad = jnp.sum(moe_in_grad * residual * scale_two, axis=0)
    residual_grad = grad_full + norm_back(residual, scale_two, norm_gain_moe, moe_in_grad)
    branch_grad = (residual_mult * residual_grad).astype(jnp.bfloat16)
    out_weight_grad = row_contract(attended, branch_grad)
    attended_grad = times_transposed(branch_grad, w_out).astype(jnp.bfloat16)
    key_grad_all = jnp.zeros((dp_count * tokens_here, kv_here * HEAD_DIM), jnp.float32)
    value_grad_all = jnp.zeros((dp_count * tokens_here, kv_here * HEAD_DIM), jnp.float32)
    local_block = 0
    packed_query = my_blocks[local_block]
    block_reach = my_offsets[local_block]
    query_block = queries
    block_lse = lse_blocks[local_block]
    grad_heads = attended_grad.reshape(BLOCK, kv_here, head_group, HEAD_DIM)

    def delta_step(
        key_step,
        accumulated,
        packed_query=packed_query,
        block_reach=block_reach,
        query_block=query_block,
        block_lse=block_lse,
        grad_heads=grad_heads,
    ):

        def delta_live(running_total):
            key_part, value_part, row_start = key_block(packed_query, key_step)
            prob_block = jnp.exp(
                block_scores(query_block, key_part, key_step) - block_lse[..., None]
            )
            value_heads = value_part.reshape(BLOCK, kv_here, HEAD_DIM)
            prob_grad = jnp.einsum(
                "qhgd,khd->hgqk", grad_heads, value_heads, preferred_element_type=jnp.float32
            )
            return running_total + jnp.sum(prob_block * prob_grad, axis=-1)

        return lax.cond(
            key_step <= block_reach, delta_live, lambda running_total: running_total, accumulated
        )

    delta_sum = lax.fori_loop(
        0, window, delta_step, jnp.zeros((kv_here, head_group, BLOCK), jnp.float32)
    )

    def grad_step(
        key_step,
        grad_carry,
        packed_query=packed_query,
        block_reach=block_reach,
        query_block=query_block,
        block_lse=block_lse,
        grad_heads=grad_heads,
        delta_sum=delta_sum,
    ):
        query_acc, key_acc, value_acc = grad_carry
        key_part, value_part, row_start = key_block(packed_query, key_step)

        def grad_live(unused):
            prob_block = jnp.exp(
                block_scores(query_block, key_part, key_step) - block_lse[..., None]
            )
            query_heads = query_block.reshape(BLOCK, kv_here, head_group, HEAD_DIM)
            key_heads = key_part.reshape(BLOCK, kv_here, HEAD_DIM)
            value_heads = value_part.reshape(BLOCK, kv_here, HEAD_DIM)
            prob_grad = jnp.einsum(
                "qhgd,khd->hgqk", grad_heads, value_heads, preferred_element_type=jnp.float32
            )
            score_grad = (prob_block * (prob_grad - delta_sum[..., None])).astype(jnp.bfloat16)
            query_add = (
                jnp.einsum(
                    "hgqk,khd->qhgd", score_grad, key_heads, preferred_element_type=jnp.float32
                )
                * score_mult
            )
            key_add = (
                jnp.einsum(
                    "hgqk,qhgd->khd", score_grad, query_heads, preferred_element_type=jnp.float32
                )
                * score_mult
            )
            value_add = jnp.einsum(
                "hgqk,qhgd->khd",
                prob_block.astype(jnp.bfloat16),
                grad_heads,
                preferred_element_type=jnp.float32,
            )
            return (
                query_add,
                key_add.reshape(BLOCK, kv_here * HEAD_DIM),
                value_add.reshape(BLOCK, kv_here * HEAD_DIM),
            )

        def dead(unused):
            return (
                jnp.zeros((BLOCK, kv_here, head_group, HEAD_DIM), jnp.float32),
                jnp.zeros((BLOCK, kv_here * HEAD_DIM), jnp.float32),
                jnp.zeros((BLOCK, kv_here * HEAD_DIM), jnp.float32),
            )

        query_add, key_add, value_add = lax.cond(key_step <= block_reach, grad_live, dead, 0)
        key_acc = lax.dynamic_update_slice_in_dim(
            key_acc, lax.dynamic_slice_in_dim(key_acc, row_start, BLOCK, 0) + key_add, row_start, 0
        )
        value_acc = lax.dynamic_update_slice_in_dim(
            value_acc,
            lax.dynamic_slice_in_dim(value_acc, row_start, BLOCK, 0) + value_add,
            row_start,
            0,
        )
        return (query_acc + query_add, key_acc, value_acc)

    start_grads = (
        jnp.zeros((BLOCK, kv_here, head_group, HEAD_DIM), jnp.float32),
        key_grad_all,
        value_grad_all,
    )
    query_acc, key_grad_all, value_grad_all = lax.fori_loop(0, window, grad_step, start_grads)
    query_grad_blocks = query_acc.reshape(BLOCK, kv_here * head_group * HEAD_DIM)
    key_grad_sum, value_grad_sum = tuple(
        (
            part.astype(jnp.float32)
            for part in in_one_piece_2(
                (key_grad_all.astype(jnp.bfloat16), value_grad_all.astype(jnp.bfloat16)), "dp", 0, 1
            )
        )
    )
    query_pre_grad = rotate_back(query_grad_blocks, cosine, sine_table).astype(jnp.bfloat16)
    key_pre_grad = rotate_back(key_grad_sum, cosine, sine_table).astype(jnp.bfloat16)
    value_pre_grad = value_grad_sum.astype(jnp.bfloat16)
    normed_part = (
        times_transposed(query_pre_grad, w_query)
        + times_transposed(key_pre_grad, w_key)
        + times_transposed(value_pre_grad, w_value)
    )
    query_weight_grad = row_contract(normed, query_pre_grad)
    key_weight_grad = row_contract(normed, key_pre_grad)
    value_weight_grad = row_contract(normed, value_pre_grad)
    normed_grad = lax.psum(normed_part.astype(jnp.bfloat16), "mp").astype(jnp.float32)
    attn_gain_grad = jnp.sum(normed_grad * input_full * scale_one, axis=0)
    hidden_grad_full = residual_grad + norm_back(input_full, scale_one, norm_gain_attn, normed_grad)
    grad_hidden = lax.dynamic_slice_in_dim(hidden_grad_full, column_start, column_share, 1)
    reduced = (
        *tuple(
            (
                part.astype(jnp.float32)
                for part in in_one_piece_2(
                    (
                        query_weight_grad.astype(jnp.bfloat16),
                        key_weight_grad.astype(jnp.bfloat16),
                        value_weight_grad.astype(jnp.bfloat16),
                    ),
                    "dp",
                    0,
                    1,
                )
            )
        ),
        lax.psum_scatter(
            out_weight_grad.astype(jnp.bfloat16), "dp", scatter_dimension=1, tiled=True
        ).astype(jnp.float32),
        *tuple(
            (
                part.astype(jnp.float32)
                for part in in_one_piece_3(
                    (
                        router_grad.astype(jnp.bfloat16),
                        attn_gain_grad.astype(jnp.bfloat16),
                        moe_gain_grad.astype(jnp.bfloat16),
                    ),
                    "dp",
                    0,
                    1,
                )
            )
        ),
    )
    (
        query_reduced,
        key_reduced,
        value_reduced,
        out_reduced,
        router_reduced,
        attn_gain_reduced,
        moe_gain_reduced,
    ) = reduced
    return (
        out_hidden,
        grad_hidden,
        query_reduced,
        key_reduced,
        value_reduced,
        out_reduced,
        attn_gain_reduced,
        moe_gain_reduced,
        router_reduced,
        grad_w_gate,
        grad_w_up,
        grad_w_down,
    )


def solution(mesh):
    in_specs = (
        P("dp", None),
        P(),
        P(),
        P("dp", None),
        P(),
        P(None, "mp"),
        P(None, "mp"),
        P(None, "mp"),
        P("mp", None),
        P(),
        P(),
        P("dp", None, "mp"),
        P("dp", None, "mp"),
        P("dp", "mp", None),
        P("dp", None),
    )
    out_specs = (
        P("dp", "mp"),
        P("dp", "mp"),
        P("dp", "mp"),
        P("dp", "mp"),
        P("dp", "mp"),
        P("mp", "dp"),
        P("dp"),
        P("dp"),
        P("dp", None),
        P("dp", None, "mp"),
        P("dp", None, "mp"),
        P("dp", "mp", None),
    )
    return jax.shard_map(
        per_device, mesh=mesh, in_specs=in_specs, out_specs=out_specs, check_vma=False
    )
```

profile of v0, /device:TPU:0, one launch (start us, length us, event | category | flops | bytes accessed | tf_op | source)
XLA Modules:
  0.0 1511.5 jit_solution(7674880674339115348)
XLA Ops:
  14.5 1.9 convolution_convert_fusion.6
  19.1 192.0 %all-gather.5.cloned.1.call-done = bf16[16384,256]{0,1:T(8,128)(2,1)} async-done(((bf16[512,256]{0,1:T(8,128)(2,1)}), bf16[16384,256]{0,1:T(8,128)(2,1)}) %all-gather.5.cloned.1.call-update) | async-done | bytes 8388624 | tf_op jit(solution)/shard_map/all_gather | solution.py:26
  211.1 5.8 fusion.101
  216.9 8.5 while.68
  217.8 5.0 conditional.12
  226.3 10.1 while.69
  227.1 6.7 conditional.13
  230.3 3.4 fusion.23
  243.7 16.1 %scatter_custom_fusion = s32[5120]{0:T(1024)S(1)} fusion(s32[4096]{0:T(1024)S(1)} %bitcast.403, s32[4096]{0:T(1024)S(1)} %reshape.628, s32[]{:T(128)} %constant.196.clone.1), kind=kCustom, calls=%fused_computation.204 | custom fusion | bytes 20484 | tf_op jit(solution)/shard_map/scatter | solution.py:355
  260.1 47.8 %all-gather.9.cloned.1.call-done = bf16[2048,1024]{1,0:T(8,128)(2,1)} async-done(((bf16[512,1024]{1,0:T(8,128)(2,1)}), bf16[2048,1024]{1,0:T(8,128)(2,1)}) %all-gather.9.cloned.1.call-update) | async-done | bytes 4194320 | tf_op jit(solution)/shard_map/all_gather | solution.py:30
  307.9 3.5 convert_reduce_fusion
  313.4 5.1 gather_fusion
  318.6 3.8 broadcast_select_fusion
  322.3 7.4 all-to-all-start
  329.8 19.8 %all-gather.7.cloned.1.call-done = bf16[512,3072]{0,1:T(8,128)(2,1)} async-done(((bf16[128,3072]{0,1:T(8,128)(2,1)}), bf16[512,3072]{0,1:T(8,128)(2,1)}) %all-gather.7.cloned.1.call-update) | async-done | bytes 3145744 | tf_op jit(solution)/shard_map/all_gather | solution.py:37
  349.5 25.6 %all-to-all-done = bf16[32,40,1024]{2,1,0:T(8,128)(2,1)} async-done(((bf16[32,40,1024]{2,1,0:T(8,128)(2,1)}), bf16[32,40,1024]{2,1,0:T(8,128)(2,1)}, u32[]{:S(2)}, u32[]{:S(2)}) %all-to-all-start) | async-done | bytes 2621472 | tf_op jit(solution)/shard_map/all_to_all | solution.py:372
  375.1 3.7 fusion.73
  378.9 4.2 fusion.72
  386.7 1.9 copy.127
  388.7 6.7 all-to-all-start.1
  396.8 2.8 convert_element_type.308
  399.6 5.1 gather_fusion.2
  406.3 24.4 %all-to-all-done.1 = bf16[128,1,40,256]{3,2,1,0:T(8,128)(2,1)} async-done(((bf16[128,1,40,256]{3,2,1,0:T(8,128)(2,1)}), bf16[128,1,40,256]{3,2,1,0:T(8,128)(2,1)}, u32[]{:S(2)}, u32[]{:S(2)}) %all-to-all-start.1) | async-done | bytes 2621472 | tf_op jit(solution)/shard_map/all_to_all | solution.py:62
  430.7 15.1 gather_fusion.1
  448.1 3.3 all-to-all-start.5
  451.4 5.4 all-to-all-done.5
  458.4 15.7 %scatter_custom_fusion.1 = f32[5120]{0:T(1024)S(1)} fusion(s32[4096]{0:T(1024)} %bitcast.404, f32[4096]{0:T(1024)S(1)} %reshape.636, f32[]{:T(128)} %constant.190.clone.1), kind=kCustom, calls=%fused_computation.202 | custom fusion | bytes 20992 | tf_op jit(solution)/shard_map/scatter | solution.py:358
  474.3 2.7 multiply_convert_fusion
  477.1 38.3 %all_to_all.30 = bf16[32,40,1024]{2,1,0:T(8,128)(2,1)S(1)} all-to-all(bf16[32,40,1024]{2,1,0:T(8,128)(2,1)S(1)} %bitcast.376), channel_id=1, replica_groups=mesh['dp'=32,'mp'=4] {'dp'}, dimensions={0} | all-to-all | bytes 5242880 | tf_op jit(solution)/shard_map/all_to_all | solution.py:394
  515.4 2.5 fusion.67
  521.9 39.8 %all_to_all.31 = bf16[128,1,40,256]{3,2,1,0:T(8,128)(2,1)S(1)} all-to-all(bf16[128,1,40,256]{3,2,1,0:T(8,128)(2,1)S(1)} %bitcast.377), channel_id=1, replica_groups=mesh['dp'=32,'mp'=4] {'dp','mp'}, dimensions={0} | all-to-all | bytes 5242880 | tf_op jit(solution)/shard_map/all_to_all | solution.py:62
  561.7 17.0 %gather_fusion.3 = bf16[4096,256]{1,0:T(8,128)(2,1)} fusion(bf16[5120,256]{1,0:T(8,128)(2,1)S(1)} %bitcast.361, s32[4096]{0:T(1024)S(1)} %fusion.84), kind=kCustom, calls=%fused_computation.3.clone | custom fusion | bytes 4210688 | tf_op jit(solution)/shard_map/jit(_take)/gather | solution.py:436
  578.7 5.0 bitcast_reduce_fusion
  584.8 3.5 all-to-all-start.4
  588.7 15.6 %all-to-all-done.4 = bf16[4,512,256]{2,1,0:T(8,128)(2,1)S(1)} async-done(((bf16[4,512,256]{2,1,0:T(8,128)(2,1)}), bf16[4,512,256]{2,1,0:T(8,128)(2,1)S(1)}, u32[]{:S(2)}, u32[]{:S(2)}) %all-to-all-start.4) | async-done | bytes 1048608 | tf_op jit(solution)/shard_map/all_to_all | solution.py:80
  610.4 9.1 while.70
  611.2 5.6 conditional.14
  619.5 4.1 broadcast.300.clone
  623.6 4.1 broadcast.300
  627.8 26.1 %while.71 = (s32[]{:T(128)}, f32[512,2,2,64]{0,3,2,1:T(8,128)S(1)}, f32[16384,128]{0,1:T(8,128)}, f32[16384,128]{0,1:T(8,128)}, s32[]{:T(128)}, /*index=5*/s32[]...) while((s32[]{:T(128)}, f32[512,2,2,64]{0,3,2,1:T(8,128)S(1)}, ...), condition=%wide.region_46.49_spmd.clone, body=%wide.region_42.48_spmd.clone.sunk | while | flops 682688640 | bytes 31089692 | solution.py:570
  630.5 6.2 conditional.15
  637.0 1.9 add_dynamic-update-slice_fusion.3
  647.0 1.9 add_dynamic-update-slice_fusion.3
  653.9 6.2 convert_element_type.328
  661.2 2.5 convert_element_type.327
  663.7 7.6 pad_maximum_fusion
  672.2 225.3 %reduce-scatter.13.cloned.1.call-done = bf16[512,256]{0,1:T(8,128)(2,1)} async-done(((bf16[16384,256]{0,1:T(8,128)(2,1)}), bf16[512,256]{0,1:T(8,128)(2,1)}) %reduce-scatter.13.cloned.1.call-update) | async-done | bytes 262160 | tf_op jit(solution)/shard_map/reduce_scatter | solution.py:74
  901.8 3.8 fusion.65
  905.7 3.8 fusion.64
  909.5 3.3 fusion.63
  913.0 4.1 copy.160
  917.1 3.7 copy.173
  925.6 2.4 convolution_convert_fusion.4
  928.1 16.2 %all-reduce.4.cloned.1.call-done = bf16[512,1024]{1,0:T(8,128)(2,1)} async-done(((bf16[512,1024]{1,0:T(8,128)(2,1)}), bf16[512,1024]{1,0:T(8,128)(2,1)}) %all-reduce.4.cloned.1.call-update) | async-done | bytes 1048592 | tf_op jit(solution)/shard_map/psum | solution.py:591
  944.3 3.7 fusion.62
  952.0 2.3 copy.156
  954.3 3.0 convert_element_type.288
  957.3 3.0 fusion.45
  962.1 16.5 %reduce-scatter.17.cloned.1.call-done = bf16[1,128,1024]{2,1,0:T(8,128)(2,1)} async-done(((bf16[1,512,1024]{2,1,0:T(8,128)(2,1)}), bf16[1,128,1024]{2,1,0:T(8,128)(2,1)}) %reduce-scatter.17.cloned.1.call-update) | async-done | bytes 262160 | tf_op jit(solution)/shard_map/reduce_scatter | solution.py:414
  980.5 38.7 %reduce-scatter.23.cloned.1.call-done = bf16[128,2048]{1,0:T(8,128)(2,1)} async-done(((bf16[512,2048]{1,0:T(8,128)(2,1)}), bf16[128,2048]{1,0:T(8,128)(2,1)}) %reduce-scatter.23.cloned.1.call-update) | async-done | bytes 524304
  1025.5 156.3 %reduce-scatter.15.cloned.1.call-done = bf16[256,32]{0,1:T(8,128)(2,1)} async-done(((bf16[256,1024]{0,1:T(8,128)(2,1)}), bf16[256,32]{0,1:T(8,128)(2,1)}) %reduce-scatter.15.cloned.1.call-update) | async-done | bytes 16400 | tf_op jit(solution)/shard_map/reduce_scatter | solution.py:611
  1183.2 2.3 dynamic-slice_add_fusion
  1185.5 154.9 %reduce-scatter.21.cloned.1.call-done = bf16[32,34]{1,0:T(8,128)(2,1)} async-done(((bf16[1024,34]{1,0:T(8,128)(2,1)}), bf16[32,34]{1,0:T(8,128)(2,1)}) %reduce-scatter.21.cloned.1.call-update) | async-done | bytes 2192
  1343.3 157.2 %reduce-scatter.19.cloned.1.call-done = bf16[32,512]{1,0:T(8,128)(2,1)} async-done(((bf16[1024,512]{1,0:T(8,128)(2,1)}), bf16[32,512]{1,0:T(8,128)(2,1)}) %reduce-scatter.19.cloned.1.call-update) | async-done | bytes 32784
  (396 shorter events, 101.9 us)
Async XLA Ops:
  7.2 231.1 %copy-start = (bf16[256,1024]{1,0:T(8,128)(2,1)S(1)}, bf16[256,1024]{1,0:T(8,128)(2,1)}, u32[]{:S(2)}) copy-start(bf16[256,1024]{1,0:T(8,128)(2,1)} %param.43) | copy-start | bytes 1572868
  7.2 9.2 copy-start.9
  7.2 9.2 copy-start.67
  7.2 9.2 copy-start.37
  7.2 203.9 %all-gather.5.cloned.1.call-start = ((), (), s32[]{:S(2)}) async-start(), calls=%async_computation.12 | async-start | bytes 8650752 | tf_op jit(solution)/shard_map/all_gather | solution.py:26
  11.1 7.2 copy-start.59
  14.4 3.8 copy-start.69
  14.5 3.9 copy-start.33
  17.3 1.7 copy-start.24
  17.3 1.7 copy-start.26
  18.2 289.7 %all-gather.9.cloned.1.call-start = ((), (), s32[]{:S(2)}) async-start(), calls=%async_computation.18 | async-start | bytes 5242880 | tf_op jit(solution)/shard_map/all_gather | solution.py:30
  236.4 4.6 copy-start.48
  236.4 4.6 copy-start.64
  236.4 3.5 copy-start.42
  236.4 3.6 copy-start.43
  236.4 3.6 copy-start.44
  238.3 2.7 copy-start.35
  239.8 109.7 %all-gather.7.cloned.1.call-start = ((), (), s32[]{:S(2)}) async-start(), calls=%async_computation.13 | async-start | bytes 3932160 | tf_op jit(solution)/shard_map/all_gather | solution.py:37
  260.1 58.5 %copy-start.57 = (pred[1280]{0:T(1024)(128)(4,1)}, pred[1280]{0:T(1024)(128)(4,1)S(1)}, u32[]{:S(2)}) copy-start(pred[1280]{0:T(1024)(128)(4,1)S(1)} %compare_and_fusion.5) | copy-start | bytes 3844
  307.9 3.5 copy-start.10
  311.4 1.7 copy-start.53
  313.3 92.4 %copy-start.11 = (bf16[512,1024]{1,0:T(8,128)(2,1)}, bf16[512,1024]{1,0:T(8,128)(2,1)S(1)}, u32[]{:S(2)}) copy-start(bf16[512,1024]{1,0:T(8,128)(2,1)S(1)} %multiply_convert_fusion.2) | copy-start | bytes 3145732
  322.3 52.8 %all-to-all-start = ((bf16[32,40,1024]{2,1,0:T(8,128)(2,1)}), bf16[32,40,1024]{2,1,0:T(8,128)(2,1)}, u32[]{:S(2)}, u32[]{:S(2)}) async-start(bf16[32,40,1024]{2,1,0:T(8,128)(2,1)} %bitcast.375), calls=%async_computation | async-start | bytes 5242880 | tf_op jit(solution)/shard_map/all_to_all | solution.py:372
  375.1 3.7 copy-start.30
  378.9 4.2 copy-start.16
  388.7 42.1 %all-to-all-start.1 = ((bf16[128,1,40,256]{3,2,1,0:T(8,128)(2,1)}), bf16[128,1,40,256]{3,2,1,0:T(8,128)(2,1)}, u32[]{:S(2)}, u32[]{:S(2)}) async-start(bf16[128,1,40,256]{3,2,1,0:T(8,128)(2,1)} %bitcast.374), calls=%async_computation.1 | async-start | bytes 5242880 | tf_op jit(solution)/shard_map/all_to_all | solution.py:62
  399.6 6.2 copy-start.36
  405.8 40.1 %copy-start.50 = (pred[4096]{0:T(1024)(128)(4,1)}, pred[4096]{0:T(1024)(128)(4,1)S(1)}, u32[]{:S(2)}) copy-start(pred[4096]{0:T(1024)(128)(4,1)S(1)} %compare_and_fusion.4) | copy-start | bytes 12292
  406.3 45.1 %copy-start.58 = (f32[512]{0:T(512)}, f32[512]{0:T(512)S(1)}, u32[]{:S(2)}) copy-start(f32[512]{0:T(512)S(1)} %reduce_max.18) | copy-start | bytes 6148
  445.8 31.2 %copy-start.7 = (bf16[4096,256]{1,0:T(8,128)(2,1)}, bf16[4096,256]{1,0:T(8,128)(2,1)S(1)}, u32[]{:S(2)}) copy-start(bf16[4096,256]{1,0:T(8,128)(2,1)S(1)} %gather_fusion.1) | copy-start | bytes 6291460
  448.1 8.7 all-to-all-start.5
  458.2 18.8 %copy-start.22 = (f32[512,8]{1,0:T(8,128)}, f32[512,8]{1,0:T(8,128)S(1)}, u32[]{:S(2)}) copy-start(f32[512,8]{1,0:T(8,128)S(1)} %copy.120) | copy-start | bytes 49156
  474.3 41.0 %copy-start.31 = (bf16[512,3072]{0,1:T(8,128)(2,1)S(1)}, bf16[512,3072]{0,1:T(8,128)(2,1)}, u32[]{:S(2)}) copy-start(bf16[512,3072]{0,1:T(8,128)(2,1)} %all-gather.7.cloned.1.call-done) | copy-start | bytes 9437188
  477.1 38.3 %copy-start.17 = (f32[512,32,40]{0,2,1:T(8,128)S(1)}, f32[512,32,40]{0,2,1:T(8,128)}, u32[]{:S(2)}) copy-start(f32[512,32,40]{0,2,1:T(8,128)} %copy-done.16) | copy-start | bytes 7864324
  477.1 38.3 %copy-start.19 = (f32[512,32,40]{0,2,1:T(8,128)S(1)}, f32[512,32,40]{0,2,1:T(8,128)}, u32[]{:S(2)}) copy-start(f32[512,32,40]{0,2,1:T(8,128)} %copy-done.18) | copy-start | bytes 7864324
  515.4 2.5 copy-start.12
  561.7 17.0 %copy-start.51 = (pred[4096]{0:T(1024)(128)(4,1)S(1)}, pred[4096]{0:T(1024)(128)(4,1)}, u32[]{:S(2)}) copy-start(pred[4096]{0:T(1024)(128)(4,1)} %copy-done.50) | copy-start | bytes 12292
  578.7 9.9 copy-start.63
  584.8 19.5 %all-to-all-start.4 = ((bf16[4,512,256]{2,1,0:T(8,128)(2,1)}), bf16[4,512,256]{2,1,0:T(8,128)(2,1)S(1)}, u32[]{:S(2)}, u32[]{:S(2)}) async-start(bf16[4,512,256]{2,1,0:T(8,128)(2,1)} %broadcast_in_dim.218), calls=%async_computation.4 | async-start | bytes 2097152 | tf_op jit(solution)/shard_map/all_to_all | solution.py:80
  588.4 309.2 %reduce-scatter.13.cloned.1.call-start = ((), (), s32[]{:S(2)}) async-start(), calls=%async_computation.14 | async-start | bytes 8650752 | tf_op jit(solution)/shard_map/reduce_scatter | solution.py:74
  613.6 1.8 copy-start.45
  630.8 2.0 copy-start.46
  653.9 7.3 copy-start.2
  671.3 227.4 %copy-start.38 = (bf16[1024,128]{1,0:T(8,128)(2,1)S(1)}, bf16[1024,128]{1,0:T(8,128)(2,1)}, u32[]{:S(2)}) copy-start(bf16[1024,128]{1,0:T(8,128)(2,1)} %param.41) | copy-start | bytes 786436
  671.3 273.0 %all-reduce.4.cloned.1.call-start = ((), (), s32[]{:S(2)}) async-start(), calls=%async_computation.15 | async-start | bytes 2097152 | tf_op jit(solution)/shard_map/psum | solution.py:591
  672.1 227.0 %copy-start.39 = (bf16[1024,128]{1,0:T(8,128)(2,1)S(1)}, bf16[1024,128]{1,0:T(8,128)(2,1)}, u32[]{:S(2)}) copy-start(bf16[1024,128]{1,0:T(8,128)(2,1)} %param.42) | copy-start | bytes 786436
  899.7 2.1 copy-start.13
  901.2 77.4 %reduce-scatter.17.cloned.1.call-start = ((), (), s32[]{:S(2)}) async-start(), calls=%async_computation.17 | async-start | bytes 1310720 | tf_op jit(solution)/shard_map/reduce_scatter | solution.py:414
  905.6 3.8 copy-start.29
  905.6 113.5 %reduce-scatter.23.cloned.1.call-start = ((), (), s32[]{:S(2)}) async-start(), calls=%async_computation.21 | async-start | bytes 2621440
  917.1 3.8 copy-start.6
  917.1 3.8 copy-start.21
  920.8 3.0 copy-start.60
  920.8 3.0 copy-start.68
  920.8 261.1 %reduce-scatter.15.cloned.1.call-start = ((), (), s32[]{:S(2)}) async-start(), calls=%async_computation.16 | async-start | bytes 540672 | tf_op jit(solution)/shard_map/reduce_scatter | solution.py:611
  922.2 418.1 %reduce-scatter.21.cloned.1.call-start = ((), (), s32[]{:S(2)}) async-start(), calls=%async_computation.20 | async-start | bytes 270336
  928.1 21.1 %copy-start.41 = (bf16[512,256]{0,1:T(8,128)(2,1)S(1)}, bf16[512,256]{0,1:T(8,128)(2,1)}, u32[]{:S(2)}) copy-start(bf16[512,256]{0,1:T(8,128)(2,1)} %reduce-scatter.13.cloned.1.call-done) | copy-start | bytes 786436
  928.1 22.8 %copy-start.47 = (bf16[1024,128]{0,1:T(8,128)(2,1)S(1)}, bf16[1024,128]{0,1:T(8,128)(2,1)}, u32[]{:S(2)}) copy-start(bf16[1024,128]{0,1:T(8,128)(2,1)} %convolution_convert_fusion.4) | copy-start | bytes 786436
  948.9 551.6 %reduce-scatter.19.cloned.1.call-start = ((), (), s32[]{:S(2)}) async-start(), calls=%async_computation.19 | async-start | bytes 1081344
  954.3 3.1 copy-start.23
  954.3 3.1 copy-start.52
  954.3 3.0 copy-start.8
  1020.5 162.6 %copy-start.66 = (f32[512]{0:T(512)S(1)}, f32[512]{0:T(512)}, u32[]{:S(2)}) copy-start(f32[512]{0:T(512)} %get-tuple-element.1329) | copy-start | bytes 6148
  1022.1 482.4 %copy-start.1 = (bf16[256,1024]{1,0:T(8,128)(2,1)S(1)}, bf16[256,1024]{1,0:T(8,128)(2,1)}, u32[]{:S(2)}) copy-start(bf16[256,1024]{1,0:T(8,128)(2,1)} %param.43) | copy-start | bytes 1572868
  (20 other events, 25.2 us)
Sparse Core Ops, SparseCore 0:
  18.3 192.7 all-gather.4
  239.9 67.8 all-gather.8
  309.5 39.9 all-gather.6
  671.4 226.1 reduce-scatter.12
  901.3 42.9 all-reduce.3
  947.0 31.6 reduce-scatter.16
  981.3 37.7 reduce-scatter.22
  1022.1 159.6 reduce-scatter.14
  1184.2 156.0 reduce-scatter.20
  1342.6 157.8 reduce-scatter.18
where the time goes:
time: 1520 us; the launch traced here: 1510 us
  waiting for transfers between devices  1100 us (72%)
  local copies, waits for them, and re-layouts  138 us (9%)
  other arithmetic  85 us (6%)
  blocking collectives  78 us (5%)
  matrix products  55.7 us (4%)
  starting transfers between devices  22 us (1%)
  loops' own time  20.3 us (1%)
  between operations  16.3 us (1%)
    unnamed x13, waiting for transfers between devices  351 us
    reduce_scatter x1, waiting for transfers between devices, in_one_piece_2(): lax.psum_scatter(both, axis, scatter_dimension=dim, tiled=True)  225 us
    all_gather x1, waiting for transfers between devices, in_one_piece(): lax.all_gather(both, axis, axis=dim, tiled=True)  192 us
    reduce_scatter x1, waiting for transfers between devices, per_device(): lax.psum_scatter(out_weight_grad.astype(jnp.bfloat16), 'dp', scatter_dime...  156 us
    all_gather x1, waiting for transfers between devices, gathered_total(): parts = lax.all_gather(x, axis).astype(jnp.float32)  47.8 us
    all_to_all x1, blocking collectives, exchange_both(): parts = lax.all_to_all(parts, axis, split_axis=0, concat_axis=0, tiled=True)  39.8 us
    all_to_all x1, blocking collectives, per_device(): lax.all_to_all(outgoing_grad, 'dp', split_axis=0, concat_axis=0, tiled=True)  38.3 us
  transfers between devices with their start and end apart: 14, of which 14 were waited for; matrix products, arithmetic and copies ran while one was open for 7% of the time, Pallas kernels for 0%

commit v1 on v0

--- a/solution.py
+++ b/solution.py
@@ -94,6 +94,24 @@
         finished.append(share.reshape(*share.shape[:along], *a.shape[along:]))
         at += column.shape[along]
     return tuple(finished)
+
+
+def from_peers(x, axis):
+    got = [x]
+    for flip in (1, 2, 3):
+        got.append(lax.ppermute(x, axis, [(i, i ^ flip) for i in range(4)]))
+    return got
+
+
+def in_mesh_order(parts, rank, dim):
+    stacked = jnp.stack(parts)
+    order = jnp.arange(4, dtype=jnp.int32) ^ rank
+    return laid_out(jnp.take(stacked, order, axis=0), dim)
+
+
+def reduced_share(x, axis):
+    parts = lax.all_to_all(x, axis, 0, 0, tiled=True)
+    return jnp.sum(parts.astype(jnp.float32), axis=0)
 
 
 def rms_scale(row_values):
@@ -253,16 +271,33 @@
     queries = rotate(query_pre, cosine, sine_table).astype(jnp.bfloat16)
     key_rows = rotate(key_pre, cosine, sine_table).astype(jnp.bfloat16)
     value_rows = value_pre.astype(jnp.bfloat16)
-    keys_all, values_all = in_one_piece((key_rows, value_rows), "dp", 0, 1)
+    piece = BLOCK // dp_count
+    kv_width = key_rows.shape[1] + value_rows.shape[1]
+    key_value = jnp.concatenate([key_rows, value_rows], axis=1)
+    spread = lax.all_to_all(
+        key_value.reshape(dp_count, piece, kv_width), "dp", 0, 0, tiled=True
+    )
+    back_steps = jnp.arange(1, window, dtype=jnp.int32)
+    wanted = jnp.maximum(block_order[:, None] - back_steps[None, :], 0)
+    wanted_from = jnp.sum(
+        jnp.where(wanted[:, :, None] == block_ids[None, None, :], inverse[None, None, :], 0), axis=2
+    )
+    picked_kv = jnp.take(spread, wanted_from.reshape(-1), axis=0)
+    earlier = lax.all_to_all(
+        picked_kv.reshape(dp_count, (window - 1) * piece, kv_width), "dp", 0, 0, tiled=True
+    )
+    earlier = jnp.moveaxis(earlier.reshape(dp_count, window - 1, piece, kv_width), 1, 0)
+    kv_window = jnp.concatenate(
+        [key_value[None], earlier.reshape(window - 1, BLOCK, kv_width)], axis=0
+    )
+    keys_window = kv_window[:, :, : key_rows.shape[1]]
+    values_window = kv_window[:, :, key_rows.shape[1] :]
 
     def key_block(packed_query, key_step):
-        packed_key = jnp.maximum(packed_query - key_step, 0)
-        source = jnp.sum(jnp.where(block_ids == packed_key, inverse, 0))
-        row_start = source * BLOCK
         return (
-            lax.dynamic_slice_in_dim(keys_all, row_start, BLOCK, 0),
-            lax.dynamic_slice_in_dim(values_all, row_start, BLOCK, 0),
-            row_start,
+            lax.dynamic_index_in_dim(keys_window, key_step, 0, False),
+            lax.dynamic_index_in_dim(values_window, key_step, 0, False),
+            key_step,
         )
 
     def block_scores(query_block, key_block_rows, key_step):
@@ -336,7 +371,11 @@
     lse_blocks = [block_lse]
     attended = attended_blocks.astype(jnp.bfloat16)
     branch_part = jnp.dot(attended, w_out, preferred_element_type=jnp.float32)
-    branch = gathered_total(branch_part.astype(jnp.bfloat16), "mp").astype(jnp.float32)
+    branch_sent = jnp.moveaxis(
+        branch_part.astype(jnp.bfloat16).reshape(tokens_here, mp_count, column_share), 1, 0
+    )
+    branch_own = reduced_share(branch_sent, "mp").astype(jnp.bfloat16)
+    branch = in_mesh_order(from_peers(branch_own, "mp"), mp_rank, 1).astype(jnp.float32)
     residual = input_full + residual_mult * branch
     scale_two = rms_scale(residual)
     moe_in = (residual * scale_two * norm_gain_moe).astype(jnp.bfloat16)
@@ -437,13 +476,12 @@
         input_home.reshape(EXPERTS * capacity, column_share), pair_slot, axis=0
     ).reshape(tokens_here, route_width, column_share)
     expert_grad_cols = jnp.sum(home_rows.astype(jnp.float32), axis=1)
-    expert_grad, gate_parts = (
-        gathered_copies(expert_grad_cols.astype(jnp.bfloat16), "mp", 1).astype(
-            expert_grad_cols.dtype
-        ),
-        gathered_copies(gate_part.astype(jnp.bfloat16), "mp", 1).astype(gate_part.dtype),
-    )
-    gate_total = jnp.sum(gate_parts.reshape(tokens_here, mp_count, route_width), axis=1)
+    expert_grad = in_mesh_order(
+        from_peers(expert_grad_cols.astype(jnp.bfloat16), "mp"), mp_rank, 1
+    ).astype(jnp.float32)
+    gate_total = sum(
+        part.astype(jnp.float32) for part in from_peers(gate_part.astype(jnp.bfloat16), "mp")
+    )
     select_grad = gate_weights * (
         gate_total - jnp.sum(gate_weights * gate_total, axis=-1, keepdims=True)
     )
@@ -457,8 +495,8 @@
     branch_grad = (residual_mult * residual_grad).astype(jnp.bfloat16)
     out_weight_grad = row_contract(attended, branch_grad)
     attended_grad = times_transposed(branch_grad, w_out).astype(jnp.bfloat16)
-    key_grad_all = jnp.zeros((dp_count * tokens_here, kv_here * HEAD_DIM), jnp.float32)
-    value_grad_all = jnp.zeros((dp_count * tokens_here, kv_here * HEAD_DIM), jnp.float32)
+    key_grad_all = jnp.zeros((window, BLOCK, kv_here * HEAD_DIM), jnp.float32)
+    value_grad_all = jnp.zeros((window, BLOCK, kv_here * HEAD_DIM), jnp.float32)
     local_block = 0
     packed_query = my_blocks[local_block]
     block_reach = my_offsets[local_block]
@@ -551,15 +589,8 @@
             )
 
         query_add, key_add, value_add = lax.cond(key_step <= block_reach, grad_live, dead, 0)
-        key_acc = lax.dynamic_update_slice_in_dim(
-            key_acc, lax.dynamic_slice_in_dim(key_acc, row_start, BLOCK, 0) + key_add, row_start, 0
-        )
-        value_acc = lax.dynamic_update_slice_in_dim(
-            value_acc,
-            lax.dynamic_slice_in_dim(value_acc, row_start, BLOCK, 0) + value_add,
-            row_start,
-            0,
-        )
+        key_acc = lax.dynamic_update_index_in_dim(key_acc, key_add, row_start, 0)
+        value_acc = lax.dynamic_update_index_in_dim(value_acc, value_add, row_start, 0)
         return (query_acc + query_add, key_acc, value_acc)
 
     start_grads = (
@@ -569,14 +600,27 @@
     )
     query_acc, key_grad_all, value_grad_all = lax.fori_loop(0, window, grad_step, start_grads)
     query_grad_blocks = query_acc.reshape(BLOCK, kv_here * head_group * HEAD_DIM)
-    key_grad_sum, value_grad_sum = tuple(
-        (
-            part.astype(jnp.float32)
-            for part in in_one_piece_2(
-                (key_grad_all.astype(jnp.bfloat16), value_grad_all.astype(jnp.bfloat16)), "dp", 0, 1
-            )
-        )
-    )
+    kv_grads = jnp.concatenate([key_grad_all, value_grad_all], axis=2)
+    later_grads = kv_grads[1:].astype(jnp.bfloat16)
+    later_grads = later_grads.reshape(window - 1, dp_count, piece, kv_width)
+    later_grads = jnp.moveaxis(later_grads, 1, 0).reshape(dp_count, -1, kv_width)
+    gathered_grads = lax.all_to_all(later_grads, "dp", 0, 0, tiled=True)
+    after = block_order[:, None] + back_steps[None, :]
+    after_hit = after[:, :, None] == block_ids[None, None, :]
+    after_from = jnp.sum(jnp.where(after_hit, inverse[None, None, :], 0), axis=2)
+    after_reach = jnp.sum(jnp.where(after_hit, offsets[None, None, :], 0), axis=2)
+    after_live = after_reach >= back_steps[None, :]
+    rows_of = (after_from * (window - 1) + back_steps[None, :] - 1).reshape(-1)
+    taken = jnp.take(
+        gathered_grads.reshape(dp_count * (window - 1), piece, kv_width), rows_of, axis=0
+    ).reshape(dp_count, window - 1, piece, kv_width)
+    summed = jnp.sum(
+        jnp.where(after_live[:, :, None, None], taken.astype(jnp.float32), 0.0), axis=1
+    )
+    home = lax.all_to_all(summed.astype(jnp.bfloat16), "dp", 0, 0, tiled=True)
+    kv_grad_sum = kv_grads[0] + home.reshape(BLOCK, kv_width).astype(jnp.float32)
+    key_grad_sum = kv_grad_sum[:, : key_rows.shape[1]]
+    value_grad_sum = kv_grad_sum[:, key_rows.shape[1] :]
     query_pre_grad = rotate_back(query_grad_blocks, cosine, sine_table).astype(jnp.bfloat16)
     key_pre_grad = rotate_back(key_grad_sum, cosine, sine_table).astype(jnp.bfloat16)
     value_pre_grad = value_grad_sum.astype(jnp.bfloat16)
@@ -588,44 +632,52 @@
     query_weight_grad = row_contract(normed, query_pre_grad)
     key_weight_grad = row_contract(normed, key_pre_grad)
     value_weight_grad = row_contract(normed, value_pre_grad)
-    normed_grad = lax.psum(normed_part.astype(jnp.bfloat16), "mp").astype(jnp.float32)
+    normed_sent = jnp.moveaxis(
+        normed_part.astype(jnp.bfloat16).reshape(tokens_here, mp_count, column_share), 1, 0
+    )
+    normed_own = reduced_share(normed_sent, "mp").astype(jnp.bfloat16)
+    normed_grad = in_mesh_order(from_peers(normed_own, "mp"), mp_rank, 1).astype(jnp.float32)
     attn_gain_grad = jnp.sum(normed_grad * input_full * scale_one, axis=0)
     hidden_grad_full = residual_grad + norm_back(input_full, scale_one, norm_gain_attn, normed_grad)
     grad_hidden = lax.dynamic_slice_in_dim(hidden_grad_full, column_start, column_share, 1)
+    def share_rows(x):
+        return x.astype(jnp.bfloat16).reshape(dp_count, x.shape[0] // dp_count, -1)
+
+    early = reduced_share(
+        jnp.concatenate(
+            [
+                share_rows(out_weight_grad.T),
+                share_rows(router_grad),
+                share_rows(moe_gain_grad[:, None]),
+            ],
+            axis=2,
+        ),
+        "dp",
+    )
+    late = reduced_share(
+        jnp.concatenate(
+            [
+                share_rows(query_weight_grad),
+                share_rows(key_weight_grad),
+                share_rows(value_weight_grad),
+                share_rows(attn_gain_grad[:, None]),
+            ],
+            axis=2,
+        ),
+        "dp",
+    )
+    q_end = query_weight_grad.shape[1]
+    k_end = q_end + key_weight_grad.shape[1]
+    v_end = k_end + value_weight_grad.shape[1]
+    o_end = out_weight_grad.shape[0]
     reduced = (
-        *tuple(
-            (
-                part.astype(jnp.float32)
-                for part in in_one_piece_2(
-                    (
-                        query_weight_grad.astype(jnp.bfloat16),
-                        key_weight_grad.astype(jnp.bfloat16),
-                        value_weight_grad.astype(jnp.bfloat16),
-                    ),
-                    "dp",
-                    0,
-                    1,
-                )
-            )
-        ),
-        lax.psum_scatter(
-            out_weight_grad.astype(jnp.bfloat16), "dp", scatter_dimension=1, tiled=True
-        ).astype(jnp.float32),
-        *tuple(
-            (
-                part.astype(jnp.float32)
-                for part in in_one_piece_3(
-                    (
-                        router_grad.astype(jnp.bfloat16),
-                        attn_gain_grad.astype(jnp.bfloat16),
-                        moe_gain_grad.astype(jnp.bfloat16),
-                    ),
-                    "dp",
-                    0,
-                    1,
-                )
-            )
-        ),
+        late[:, :q_end],
+        late[:, q_end:k_end],
+        late[:, k_end:v_end],
+        early[:, :o_end].T,
+        early[:, o_end : o_end + EXPERTS],
+        late[:, v_end],
+        early[:, o_end + EXPERTS],
     )
     (
         query_reduced,

time: 1520 us -> 702 us (0.46)
  the two profiles are of different devices: /device:TPU:0 before, /device:TPU:1 now
where the time goes in v1:
time: 702 us; the launch traced here: 690 us
  local copies, waits for them, and re-layouts  160 us (23%)
  starting transfers between devices  138 us (20%)
  waiting for transfers between devices  126 us (18%)
  blocking collectives  102 us (15%)
  other arithmetic  71.6 us (10%)
  matrix products  64.3 us (9%)
  between operations  16.5 us (2%)
  loops' own time  11.5 us (2%)
    all_to_all x1, blocking collectives, per_device(): lax.all_to_all(outgoing, 'dp', split_axis=0, concat_axis=0, tiled=True)  64.6 us
    all_to_all x1, starting transfers between devices, per_device(): gathered_grads = lax.all_to_all(later_grads, 'dp', 0, 0, tiled=True)  63.9 us
    all_to_all x2, waiting for transfers between devices, exchange_both(): parts = lax.all_to_all(parts, axis, split_axis=0, concat_axis=0, tiled=True)  43.3 us
    all_to_all x1, blocking collectives, per_device(): lax.all_to_all(outgoing_grad, 'dp', split_axis=0, concat_axis=0, tiled=True)  37.7 us
    ppermute x12, waiting for transfers between devices, from_peers(): got.append(lax.ppermute(x, axis, [(i, i ^ flip) for i in range(4)]))  27.7 us
    all_to_all x4, waiting for transfers between devices, reduced_share(): parts = lax.all_to_all(x, axis, 0, 0, tiled=True)  27.3 us
    unnamed x179, local copies, waits for them, and re-layouts  24.8 us
    all_to_all x4, starting transfers between devices, reduced_share(): parts = lax.all_to_all(x, axis, 0, 0, tiled=True)  21.2 us
  transfers between devices with their start and end apart: 25, of which 17 were waited for; matrix products, arithmetic and copies ran while one was open for 31% of the time, Pallas kernels for 0%

profile of v1, /device:TPU:1, one launch (start us, length us, event | category | flops | bytes accessed | tf_op | source)
XLA Modules:
  0.0 689.8 jit_solution(5445712835556855650)
XLA Ops:
  18.2 9.8 %all-to-all-start = ((bf16[32,16,256]{2,1,0:T(8,128)(2,1)}), bf16[32,16,256]{2,1,0:T(8,128)(2,1)S(1)}, u32[]{:S(2)}, u32[]{:S(2)}) async-start(bf16[32,16,256]{2,1,0:T(8,128)(2,1)} %bitcast.47), calls=%async_computation | async-start | bytes 524288 | tf_op jit(solution)/shard_map/all_to_all | solution.py:277
  33.8 2.8 all-to-all-done
  39.2 4.9 all-to-all-start.1
  47.8 19.2 %all-to-all-done.1 = bf16[32,48,256]{2,1,0:T(8,128)(2,1)S(1)} async-done(((bf16[32,48,256]{2,1,0:T(8,128)(2,1)}), bf16[32,48,256]{2,1,0:T(8,128)(2,1)S(1)}, u32[]{:S(2)}, u32[]{:S(2)}) %all-to-all-start.1) | async-done | bytes 786464 | tf_op jit(solution)/shard_map/all_to_all | solution.py:286
  69.0 6.6 while.68
  69.9 3.0 conditional.12
  78.4 9.7 %while.69 = (s32[]{:T(128)}, f32[512,2,2,64]{0,3,2,1:T(8,128)}, s32[]{:T(128)}, bf16[4,512,128]{1,2,0:T(8,128)(2,1)S(1)}, bf16[4,512,128]{1,2,0:T(8,128)(2,1)}, ...) while((s32[]{:T(128)}, f32[512,2,2,64]{0,3,2,1:T(8,128)}, s32[]{:T(128)}, ...), condition=%wide.region_16.17_spmd.clone, body=%wide.region_13.16_spmd.clone.sunk | while | flops 273285120 | bytes 6824155 | solution.py:367
  79.2 6.1 conditional.13
  81.8 3.6 fusion.14
  91.6 6.8 all-to-all-start.2
  98.6 15.8 %scatter_custom_fusion = s32[5120]{0:T(1024)S(1)} fusion(s32[4096]{0:T(1024)S(1)} %bitcast.483, s32[4096]{0:T(1024)S(1)} %reshape.862, s32[]{:T(128)} %constant.244.clone.1), kind=kCustom, calls=%fused_computation.220 | custom fusion | bytes 20484 | tf_op jit(solution)/shard_map/scatter | solution.py:394
  115.0 3.2 collective-permute-start.1
  118.7 5.8 collective-permute-done.1
  124.5 6.0 collective-permute-done.2
  134.8 5.1 gather_fusion.3
  142.0 64.6 %all_to_all.60 = bf16[32,40,1024]{2,1,0:T(8,128)(2,1)} all-to-all(bf16[32,40,1024]{2,1,0:T(8,128)(2,1)S(1)} %bitcast.431), channel_id=1, replica_groups=mesh['dp'=32,'mp'=4] {'dp'}, dimensions={0} | all-to-all | bytes 5242880 | tf_op jit(solution)/shard_map/all_to_all | solution.py:411
  206.6 3.7 fusion.60
  217.3 8.1 %all-to-all-start.4 = ((bf16[128,1,40,256]{3,2,1,0:T(8,128)(2,1)}), bf16[128,1,40,256]{3,2,1,0:T(8,128)(2,1)}, u32[]{:S(2)}, u32[]{:S(2)}) async-start(bf16[128,1,40,256]{3,2,1,0:T(8,128)(2,1)} %bitcast.429), calls=%async_computation.4 | async-start | bytes 5242880 | tf_op jit(solution)/shard_map/all_to_all | solution.py:62
  227.3 5.1 gather_fusion.5
  234.7 26.2 %all-to-all-done.4 = bf16[128,1,40,256]{3,2,1,0:T(8,128)(2,1)} async-done(((bf16[128,1,40,256]{3,2,1,0:T(8,128)(2,1)}), bf16[128,1,40,256]{3,2,1,0:T(8,128)(2,1)}, u32[]{:S(2)}, u32[]{:S(2)}) %all-to-all-start.4) | async-done | bytes 2621472 | tf_op jit(solution)/shard_map/all_to_all | solution.py:62
  260.8 15.1 %gather_fusion.4 = bf16[4096,256]{1,0:T(8,128)(2,1)S(1)} fusion(bf16[5120,256]{1,0:T(8,128)(2,1)} %bitcast.95, s32[4096]{0:T(1024)S(1)} %fusion.72), kind=kCustom, calls=%fused_computation.2.clone | custom fusion | bytes 4210688 | tf_op jit(solution)/shard_map/jit(_take)/gather | solution.py:465
  285.9 15.7 %scatter_custom_fusion.1 = f32[5120]{0:T(1024)S(1)} fusion(s32[4096]{0:T(1024)} %bitcast.484, f32[4096]{0:T(1024)S(1)} %reshape.870, f32[]{:T(128)} %constant.238.clone.1), kind=kCustom, calls=%fused_computation.218 | custom fusion | bytes 20992 | tf_op jit(solution)/shard_map/scatter | solution.py:397
  301.9 2.7 multiply_convert_fusion
  304.6 37.7 %all_to_all.61 = bf16[32,40,1024]{2,1,0:T(8,128)(2,1)S(1)} all-to-all(bf16[32,40,1024]{2,1,0:T(8,128)(2,1)S(1)} %bitcast.430), channel_id=1, replica_groups=mesh['dp'=32,'mp'=4] {'dp'}, dimensions={0} | all-to-all | bytes 5242880 | tf_op jit(solution)/shard_map/all_to_all | solution.py:433
  342.4 2.5 fusion.55
  350.5 6.1 all-to-all-start.6
  356.7 2.8 convert_element_type.291
  366.8 2.1 convolution_convert_fusion.7
  370.6 4.6 fusion.53
  375.3 17.1 %all-to-all-done.6 = bf16[128,1,40,256]{3,2,1,0:T(8,128)(2,1)S(1)} async-done(((bf16[128,1,40,256]{3,2,1,0:T(8,128)(2,1)}), bf16[128,1,40,256]{3,2,1,0:T(8,128)(2,1)S(1)}, u32[]{:S(2)}, u32[]{:S(2)}) %all-to-all-start.6) | async-done | bytes 2621472 | tf_op jit(solution)/shard_map/all_to_all | solution.py:62
  392.4 17.0 %gather_fusion.6 = bf16[4096,256]{1,0:T(8,128)(2,1)} fusion(bf16[5120,256]{1,0:T(8,128)(2,1)S(1)} %bitcast.416, s32[4096]{0:T(1024)S(1)} %fusion.72), kind=kCustom, calls=%fused_computation.6.clone | custom fusion | bytes 4210688 | tf_op jit(solution)/shard_map/jit(_take)/gather | solution.py:475
  409.4 5.1 bitcast_reduce_fusion
  418.9 4.3 fusion.51
  425.0 5.8 collective-permute-done.5
  437.9 11.8 %while.70 = (s32[]{:T(128)}, f32[2,2,512]{2,1,0:T(2,128)S(1)}, s32[]{:T(128)}, bf16[4,512,128]{1,2,0:T(8,128)(2,1)}, bf16[512,256]{0,1:T(8,128)(2,1)S(1)}, /*ind...) while((s32[]{:T(128)}, f32[2,2,512]{2,1,0:T(2,128)S(1)}, ...), condition=%wide.region_38.42_spmd.clone, body=%wide.region_34.41_spmd.clone.sunk | while | flops 274202624 | bytes 15540515 | solution.py:532
  438.8 8.2 %conditional.14 = (f32[2,2,512]{2,1,0:T(2,128)S(1)}) conditional(s32[]{:T(128)} %convert_element_type.500, f32[2,2,512]{2,1,0:T(2,128)S(1)} %get-tuple-element.1444, (s32[]{:T(128)}, s32[512,512]{0,1:T(8,128)S(1)}, bf16[4,512,128]{1,2,0:T(8,128)(2,1)}, bf16[512,256]{0,1:T(8,128)(2,1)S(1)}, f32[2,2,512]{2,1,0:T(2,128)}, ...), branch_computations={%region_35.38_spmd, %region_36.40_spmd} | conditional | flops 274202624 | bytes 13443184 | solution.py:528
  439.8 2.7 fusion.100
  443.4 3.6 fusion.17
  449.7 28.0 %while.71 = (s32[]{:T(128)}, f32[512,2,2,64]{0,3,2,1:T(8,128)S(1)}, f32[4,512,128]{2,1,0:T(8,128)}, f32[4,512,128]{2,1,0:T(8,128)}, s32[]{:T(128)}, /*index=5*/b...) while((s32[]{:T(128)}, f32[512,2,2,64]{0,3,2,1:T(8,128)S(1)}, ...), condition=%wide.region_42.46_spmd.clone, body=%wide.region_39.45_spmd.clone.sunk | while | flops 682557440 | bytes 48948080 | solution.py:601
  450.6 13.1 %conditional.15 = (f32[512,2,2,64]{0,3,2,1:T(8,128)S(1)}, f32[1,512,128]{1,2,0:T(8,128)S(1)}, f32[1,512,128]{1,2,0:T(8,128)}) conditional(s32[]{:T(128)} %convert_element_type.501, () %tuple.232, (s32[]{:T(128)}, s32[512,512]{0,1:T(8,128)S(1)}, bf16[4,512,128]{1,2,0:T(8,128)(2,1)}, bf16[512,256]{0,1:T(8,128)(2,1)S(1)}, f32[2,2,512]{2,1,0:T(2,128)}, ...), branch_computations={%region_40.43_spmd, %region_41.44_spmd} | conditional | flops 682295296 | bytes 43180184 | solution.py:591
  452.2 2.7 fusion.101
  455.9 3.6 fusion.21
  481.0 63.9 %all-to-all-start.7 = ((bf16[32,48,256]{2,1,0:T(8,128)(2,1)}), bf16[32,48,256]{2,1,0:T(8,128)(2,1)}, u32[]{:S(2)}, u32[]{:S(2)}) async-start(bf16[32,48,256]{2,1,0:T(8,128)(2,1)} %bitcast.134), calls=%async_computation.7 | async-start | bytes 1572864 | tf_op jit(solution)/shard_map/all_to_all | solution.py:607
  545.1 3.0 fusion.52
  548.3 4.0 copy.228
  552.3 3.5 copy.258
  559.2 2.8 gather_fusion.1
  562.0 2.3 select_reduce_fusion
  564.3 6.6 all-to-all-start.8
  575.0 4.3 all-to-all-done.8
  579.2 3.9 all-to-all-start.11
  591.5 12.2 %all-to-all-done.11 = bf16[32,32,289]{2,1,0:T(8,128)(2,1)S(1)} async-done(((bf16[32,32,289]{2,1,0:T(8,128)(2,1)}), bf16[32,32,289]{2,1,0:T(8,128)(2,1)S(1)}, u32[]{:S(2)}, u32[]{:S(2)}) %all-to-all-start.11) | async-done | bytes 591904 | tf_op jit(solution)/shard_map/all_to_all | solution.py:113
  603.7 5.8 all-to-all-start.9
  609.6 4.3 fusion.33
  617.5 2.8 convolution_convert_fusion.2
  621.7 3.1 all-to-all-done.9
  627.3 3.4 collective-permute-start.11
  630.6 2.6 convolution_convert_fusion.3
  633.2 2.6 convolution_convert_fusion.4
  636.5 5.8 collective-permute-done.11
  643.5 2.9 gather_fusion.8
  652.9 4.7 all-to-all-start.10
  665.2 2.3 dynamic-slice_add_fusion
  667.5 12.0 %all-to-all-done.10 = bf16[32,32,513]{2,1,0:T(8,128)(2,1)} async-done(((bf16[32,32,513]{2,1,0:T(8,128)(2,1)}), bf16[32,32,513]{2,1,0:T(8,128)(2,1)}, u32[]{:S(2)}, u32[]{:S(2)}) %all-to-all-start.10) | async-done | bytes 1050656 | tf_op jit(solution)/shard_map/all_to_all | solution.py:113
  (476 shorter events, 163.7 us)
Async XLA Ops:
  7.2 82.9 %copy-start = (bf16[256,1024]{1,0:T(8,128)(2,1)S(1)}, bf16[256,1024]{1,0:T(8,128)(2,1)}, u32[]{:S(2)}) copy-start(bf16[256,1024]{1,0:T(8,128)(2,1)} %param.45) | copy-start | bytes 1572868
  7.2 9.1 %copy-start.9 = (bf16[512,1024]{1,0:T(8,128)(2,1)S(1)}, bf16[512,1024]{1,0:T(8,128)(2,1)}, u32[]{:S(2)}) copy-start(bf16[512,1024]{1,0:T(8,128)(2,1)} %param.37) | copy-start | bytes 3145732
  7.2 9.1 %copy-start.88 = (f32[1024]{0:T(1024)S(1)}, f32[1024]{0:T(1024)}, u32[]{:S(2)}) copy-start(f32[1024]{0:T(1024)} %param.41) | copy-start | bytes 12292
  7.2 9.1 %copy-start.56 = (bf16[1024,128]{1,0:T(8,128)(2,1)S(1)}, bf16[1024,128]{1,0:T(8,128)(2,1)}, u32[]{:S(2)}) copy-start(bf16[1024,128]{1,0:T(8,128)(2,1)} %param.44) | copy-start | bytes 786436
  16.3 11.8 %copy-start.60 = (bf16[1,128,1024]{2,1,0:T(8,128)(2,1)S(1)}, bf16[1,128,1024]{2,1,0:T(8,128)(2,1)}, u32[]{:S(2)}) copy-start(bf16[1,128,1024]{2,1,0:T(8,128)(2,1)} %param.50) | copy-start | bytes 786436
  16.9 11.4 %copy-start.61 = (bf16[1,1024,128]{2,1,0:T(8,128)(2,1)S(1)}, bf16[1,1024,128]{2,1,0:T(8,128)(2,1)}, u32[]{:S(2)}) copy-start(bf16[1,1024,128]{2,1,0:T(8,128)(2,1)} %param.49) | copy-start | bytes 786436
  16.9 11.4 %copy-start.62 = (bf16[1,1024,128]{2,1,0:T(8,128)(2,1)S(1)}, bf16[1,1024,128]{2,1,0:T(8,128)(2,1)}, u32[]{:S(2)}) copy-start(bf16[1,1024,128]{2,1,0:T(8,128)(2,1)} %param.48) | copy-start | bytes 786436
  17.2 30.4 %copy-start.36 = (f32[512,32]{0,1:T(8,128)}, f32[512,32]{0,1:T(8,128)S(1)}, u32[]{:S(2)}) copy-start(f32[512,32]{0,1:T(8,128)S(1)} %get-tuple-element.1156) | copy-start | bytes 196612
  17.3 30.4 %copy-start.38 = (f32[512,32]{0,1:T(8,128)}, f32[512,32]{0,1:T(8,128)S(1)}, u32[]{:S(2)}) copy-start(f32[512,32]{0,1:T(8,128)S(1)} %get-tuple-element.1157) | copy-start | bytes 196612
  17.4 11.9 %copy-start.90 = (s32[32]{0:T(128)S(1)}, s32[32]{0:T(128)}, u32[]{:S(2)}) copy-start(s32[32]{0:T(128)} %param.39) | copy-start | bytes 388
  17.4 12.7 %copy-start.52 = (s32[512,8]{0,1:T(8,128)S(1)}, s32[512,8]{0,1:T(8,128)}, u32[]{:S(2)}) copy-start(s32[512,8]{0,1:T(8,128)} %param.40) | copy-start | bytes 49156
  18.2 18.4 %all-to-all-start = ((bf16[32,16,256]{2,1,0:T(8,128)(2,1)}), bf16[32,16,256]{2,1,0:T(8,128)(2,1)S(1)}, u32[]{:S(2)}, u32[]{:S(2)}) async-start(bf16[32,16,256]{2,1,0:T(8,128)(2,1)} %bitcast.47), calls=%async_computation | async-start | bytes 524288 | tf_op jit(solution)/shard_map/all_to_all | solution.py:277
  28.1 178.5 %all-gather.2.cloned.1.call-start = ((), (), s32[]{:S(2)}) async-start(), calls=%async_computation.14 | async-start | bytes 3932160 | tf_op jit(solution)/shard_map/all_gather | solution.py:37
  37.3 6.8 copy-start.68
  37.3 9.1 %copy-start.49 = (bf16[1024,256]{1,0:T(8,128)(2,1)S(1)}, bf16[1024,256]{1,0:T(8,128)(2,1)}, u32[]{:S(2)}) copy-start(bf16[1024,256]{1,0:T(8,128)(2,1)} %param.42) | copy-start | bytes 1572868
  39.2 27.8 %all-to-all-start.1 = ((bf16[32,48,256]{2,1,0:T(8,128)(2,1)}), bf16[32,48,256]{2,1,0:T(8,128)(2,1)S(1)}, u32[]{:S(2)}, u32[]{:S(2)}) async-start(bf16[32,48,256]{2,1,0:T(8,128)(2,1)} %bitcast_select_fusion.4), calls=%async_computation.1 | async-start | bytes 1572864 | tf_op jit(solution)/shard_map/all_to_all | solution.py:286
  90.5 7.9 %copy-start.67 = (s32[4096,1]{0,1:T(1,128)S(1)}, s32[4096,1]{0,1:T(1,128)}, u32[]{:S(2)}) copy-start(s32[4096,1]{0,1:T(1,128)} %reshape.751) | copy-start | bytes 49156
  91.6 23.1 %all-to-all-start.2 = ((bf16[4,512,256]{2,1,0:T(8,128)(2,1)}), bf16[4,512,256]{2,1,0:T(8,128)(2,1)S(1)}, u32[]{:S(2)}, u32[]{:S(2)}) async-start(bf16[4,512,256]{2,1,0:T(8,128)(2,1)} %bitcast.414), calls=%async_computation.2 | async-start | bytes 2097152 | tf_op jit(solution)/shard_map/all_to_all | solution.py:113
  98.4 32.8 %copy-start.80 = (s32[4096,1]{0,1:T(1,128)}, s32[4096,1]{0,1:T(1,128)S(1)}, u32[]{:S(2)}) copy-start(s32[4096,1]{0,1:T(1,128)S(1)} %compare_select_fusion) | copy-start | bytes 49156
  114.6 16.6 %copy-start.85 = (s32[1024]{0:T(1024)}, s32[1024]{0:T(1024)S(1)}, u32[]{:S(2)}) copy-start(s32[1024]{0:T(1024)S(1)} %pad_clamp_fusion.2) | copy-start | bytes 12292
  115.0 3.8 collective-permute-start
  115.0 9.5 %collective-permute-start.1 = (bf16[512,256]{1,0:T(8,128)(2,1)S(1)}, bf16[512,256]{1,0:T(8,128)(2,1)S(1)}, u32[]{:S(2)}, u32[]{:S(2)}) collective-permute-start(bf16[512,256]{1,0:T(8,128)(2,1)S(1)} %reduce_sum.276), channel_id=1, source_target_pairs={{0,2},{1,3},{2,0},{3,1},{4,6},{5,7},{6,4},{7,5},{8,10},{9,11},{10,... | collective-permute-start | bytes 786440 | tf_op jit(solution)/shard_map/ppermute | solution.py:102
  118.3 12.2 %collective-permute-start.2 = (bf16[512,256]{1,0:T(8,128)(2,1)S(1)}, bf16[512,256]{1,0:T(8,128)(2,1)S(1)}, u32[]{:S(2)}, u32[]{:S(2)}) collective-permute-start(bf16[512,256]{1,0:T(8,128)(2,1)S(1)} %reduce_sum.276), channel_id=1, source_target_pairs={{0,3},{1,2},{2,1},{3,0},{4,7},{5,6},{6,5},{7,4},{8,11},{9,10},{10,... | collective-permute-start | bytes 786440 | tf_op jit(solution)/shard_map/ppermute | solution.py:102
  118.7 12.6 %copy-start.86 = (pred[4]{0:T(512)(128)(4,1)}, pred[4]{0:T(512)(128)(4,1)S(1)}, u32[]{:S(2)}) copy-start(pred[4]{0:T(512)(128)(4,1)S(1)} %compare_and_fusion.6) | copy-start | bytes 16
  118.7 21.2 %copy-start.75 = (pred[1280]{0:T(1024)(128)(4,1)}, pred[1280]{0:T(1024)(128)(4,1)S(1)}, u32[]{:S(2)}) copy-start(pred[1280]{0:T(1024)(128)(4,1)S(1)} %compare_and_fusion.5) | copy-start | bytes 3844
  134.7 98.8 %copy-start.12 = (bf16[512,1024]{1,0:T(8,128)(2,1)}, bf16[512,1024]{1,0:T(8,128)(2,1)S(1)}, u32[]{:S(2)}) copy-start(bf16[512,1024]{1,0:T(8,128)(2,1)S(1)} %multiply_convert_fusion.2) | copy-start | bytes 3145732
  217.3 8.2 %copy-start.29 = (s32[512,8]{1,0:T(8,128)S(1)}, s32[512,8]{1,0:T(8,128)}, u32[]{:S(2)}) copy-start(s32[512,8]{1,0:T(8,128)} %copy-done.28) | copy-start | bytes 49156
  217.3 8.3 %copy-start.16 = (bf16[512,1024]{1,0:T(8,128)(2,1)S(1)}, bf16[512,1024]{1,0:T(8,128)(2,1)}, u32[]{:S(2)}) copy-start(bf16[512,1024]{1,0:T(8,128)(2,1)} %param.51) | copy-start | bytes 3145732
  217.3 43.5 %all-to-all-start.4 = ((bf16[128,1,40,256]{3,2,1,0:T(8,128)(2,1)}), bf16[128,1,40,256]{3,2,1,0:T(8,128)(2,1)}, u32[]{:S(2)}, u32[]{:S(2)}) async-start(bf16[128,1,40,256]{3,2,1,0:T(8,128)(2,1)} %bitcast.429), calls=%async_computation.4 | async-start | bytes 5242880 | tf_op jit(solution)/shard_map/all_to_all | solution.py:62
  233.5 175.9 %copy-start.65 = (pred[4096]{0:T(1024)(128)(4,1)}, pred[4096]{0:T(1024)(128)(4,1)S(1)}, u32[]{:S(2)}) copy-start(pred[4096]{0:T(1024)(128)(4,1)S(1)} %compare_and_fusion.4) | copy-start | bytes 12292
  275.9 28.7 %copy-start.8 = (bf16[4096,256]{1,0:T(8,128)(2,1)}, bf16[4096,256]{1,0:T(8,128)(2,1)S(1)}, u32[]{:S(2)}) copy-start(bf16[4096,256]{1,0:T(8,128)(2,1)S(1)} %gather_fusion.4) | copy-start | bytes 6291460
  277.6 5.0 collective-permute-start.6
  278.6 4.0 collective-permute-start.7
  279.8 4.6 collective-permute-start.8
  285.8 18.8 %copy-start.32 = (f32[512,8]{1,0:T(8,128)}, f32[512,8]{1,0:T(8,128)S(1)}, u32[]{:S(2)}) copy-start(f32[512,8]{1,0:T(8,128)S(1)} %copy.175) | copy-start | bytes 49156
  301.9 40.5 %copy-start.43 = (bf16[512,3072]{0,1:T(8,128)(2,1)S(1)}, bf16[512,3072]{0,1:T(8,128)(2,1)}, u32[]{:S(2)}) copy-start(bf16[512,3072]{0,1:T(8,128)(2,1)} %all-gather.2.cloned.1.call-done) | copy-start | bytes 9437188
  304.6 37.7 %copy-start.23 = (f32[512,32,40]{0,2,1:T(8,128)S(1)}, f32[512,32,40]{0,2,1:T(8,128)}, u32[]{:S(2)}) copy-start(f32[512,32,40]{0,2,1:T(8,128)} %copy-done.22) | copy-start | bytes 7864324
  304.6 37.7 %copy-start.25 = (f32[512,32,40]{0,2,1:T(8,128)S(1)}, f32[512,32,40]{0,2,1:T(8,128)}, u32[]{:S(2)}) copy-start(f32[512,32,40]{0,2,1:T(8,128)} %copy-done.24) | copy-start | bytes 7864324
  350.5 42.0 %all-to-all-start.6 = ((bf16[128,1,40,256]{3,2,1,0:T(8,128)(2,1)}), bf16[128,1,40,256]{3,2,1,0:T(8,128)(2,1)S(1)}, u32[]{:S(2)}, u32[]{:S(2)}) async-start(bf16[128,1,40,256]{3,2,1,0:T(8,128)(2,1)} %bitcast.428), calls=%async_computation.6 | async-start | bytes 5242880 | tf_op jit(solution)/shard_map/all_to_all | solution.py:62
  356.6 259.2 %reduce-scatter.5.cloned.1.call-start = ((), (), s32[]{:S(2)}) async-start(), calls=%async_computation.15 | async-start | bytes 1310720 | tf_op jit(solution)/shard_map/reduce_scatter | solution.py:453
  409.4 9.5 %copy-start.41 = (bf16[32,1,40,512]{3,2,0,1:T(8,128)(2,1)S(1)}, bf16[32,1,40,512]{3,2,0,1:T(8,128)(2,1)}, u32[]{:S(2)}) copy-start(bf16[32,1,40,512]{3,2,0,1:T(8,128)(2,1)} %copy-done.40) | copy-start | bytes 3932164
  414.6 8.6 %collective-permute-start.3 = (bf16[512,256]{1,0:T(8,128)(2,1)S(1)}, bf16[512,256]{1,0:T(8,128)(2,1)S(1)}, u32[]{:S(2)}, u32[]{:S(2)}) collective-permute-start(bf16[512,256]{1,0:T(8,128)(2,1)S(1)} %bitcast_reduce_fusion), channel_id=1, source_target_pairs={{0,1},{1,0},{2,3},{3,2},{4,5},{5,4},{6,7},{7,6},{8,9},{9,8},{10,11... | collective-permute-start | bytes 786440 | tf_op jit(solution)/shard_map/ppermute | solution.py:102
  415.7 9.4 %collective-permute-start.4 = (bf16[512,256]{1,0:T(8,128)(2,1)S(1)}, bf16[512,256]{1,0:T(8,128)(2,1)S(1)}, u32[]{:S(2)}, u32[]{:S(2)}) collective-permute-start(bf16[512,256]{1,0:T(8,128)(2,1)S(1)} %bitcast_reduce_fusion), channel_id=1, source_target_pairs={{0,2},{1,3},{2,0},{3,1},{4,6},{5,7},{6,4},{7,5},{8,10},{9,11},{10,... | collective-permute-start | bytes 786440 | tf_op jit(solution)/shard_map/ppermute | solution.py:102
  416.8 14.0 %collective-permute-start.5 = (bf16[512,256]{1,0:T(8,128)(2,1)S(1)}, bf16[512,256]{1,0:T(8,128)(2,1)S(1)}, u32[]{:S(2)}, u32[]{:S(2)}) collective-permute-start(bf16[512,256]{1,0:T(8,128)(2,1)S(1)} %bitcast_reduce_fusion), channel_id=1, source_target_pairs={{0,3},{1,2},{2,1},{3,0},{4,7},{5,6},{6,5},{7,4},{8,11},{9,10},{10,... | collective-permute-start | bytes 786440 | tf_op jit(solution)/shard_map/ppermute | solution.py:102
  437.9 11.8 %copy-start.7 = (f32[512,2,2,64]{0,3,2,1:T(8,128)S(1)}, f32[512,2,2,64]{0,3,2,1:T(8,128)}, u32[]{:S(2)}) copy-start(f32[512,2,2,64]{0,3,2,1:T(8,128)} %custom-call) | copy-start | bytes 1572868
  479.4 65.7 %copy-start.27 = (bf16[32,40,1024]{2,1,0:T(8,128)(2,1)S(1)}, bf16[32,40,1024]{2,1,0:T(8,128)(2,1)}, u32[]{:S(2)}) copy-start(bf16[32,40,1024]{2,1,0:T(8,128)(2,1)} %all_to_all.60) | copy-start | bytes 7864324
  481.0 78.2 %all-to-all-start.7 = ((bf16[32,48,256]{2,1,0:T(8,128)(2,1)}), bf16[32,48,256]{2,1,0:T(8,128)(2,1)}, u32[]{:S(2)}, u32[]{:S(2)}) async-start(bf16[32,48,256]{2,1,0:T(8,128)(2,1)} %bitcast.134), calls=%async_computation.7 | async-start | bytes 1572864 | tf_op jit(solution)/shard_map/all_to_all | solution.py:607
  544.9 114.0 %reduce-scatter.7.cloned.1.call-start = ((), (), s32[]{:S(2)}) async-start(), calls=%async_computation.16 | async-start | bytes 2621440
  558.0 13.0 %copy-start.37 = (f32[512,32]{0,1:T(8,128)S(1)}, f32[512,32]{0,1:T(8,128)}, u32[]{:S(2)}) copy-start(f32[512,32]{0,1:T(8,128)} %copy-done.36) | copy-start | bytes 196612
  558.0 13.0 %copy-start.39 = (f32[512,32]{0,1:T(8,128)S(1)}, f32[512,32]{0,1:T(8,128)}, u32[]{:S(2)}) copy-start(f32[512,32]{0,1:T(8,128)} %copy-done.38) | copy-start | bytes 196612
  559.2 14.7 %copy-start.45 = (bf16[1024,32]{1,0:T(8,128)(2,1)S(1)}, bf16[1024,32]{1,0:T(8,128)(2,1)}, u32[]{:S(2)}) copy-start(bf16[1024,32]{1,0:T(8,128)(2,1)} %copy.227) | copy-start | bytes 196612
  564.3 14.9 %all-to-all-start.8 = ((bf16[32,16,256]{2,1,0:T(8,128)(2,1)}), bf16[32,16,256]{2,1,0:T(8,128)(2,1)}, u32[]{:S(2)}, u32[]{:S(2)}) async-start(bf16[32,16,256]{2,1,0:T(8,128)(2,1)} %select_reduce_fusion), calls=%async_computation.8 | async-start | bytes 524288 | tf_op jit(solution)/shard_map/all_to_all | solution.py:620
  579.2 24.5 %all-to-all-start.11 = ((bf16[32,32,289]{2,1,0:T(8,128)(2,1)}), bf16[32,32,289]{2,1,0:T(8,128)(2,1)S(1)}, u32[]{:S(2)}, u32[]{:S(2)}) async-start(bf16[32,32,289]{2,1,0:T(8,128)(2,1)} %pad_maximum_fusion.8), calls=%async_computation.11 | async-start | bytes 1572864 | tf_op jit(solution)/shard_map/all_to_all | solution.py:113
  590.5 19.1 %copy-start.33 = (f32[512,8]{1,0:T(8,128)S(1)}, f32[512,8]{1,0:T(8,128)}, u32[]{:S(2)}) copy-start(f32[512,8]{1,0:T(8,128)} %copy-done.32) | copy-start | bytes 49156
  590.5 19.1 %copy-start.66 = (pred[4096]{0:T(1024)(128)(4,1)S(1)}, pred[4096]{0:T(1024)(128)(4,1)}, u32[]{:S(2)}) copy-start(pred[4096]{0:T(1024)(128)(4,1)} %copy-done.65) | copy-start | bytes 12292
  603.7 21.0 %all-to-all-start.9 = ((bf16[4,512,256]{2,1,0:T(8,128)(2,1)}), bf16[4,512,256]{2,1,0:T(8,128)(2,1)}, u32[]{:S(2)}, u32[]{:S(2)}) async-start(bf16[4,512,256]{2,1,0:T(8,128)(2,1)} %bitcast.439), calls=%async_computation.9 | async-start | bytes 2097152 | tf_op jit(solution)/shard_map/all_to_all | solution.py:113
  609.5 8.0 %copy-start.77 = (f32[512]{0:T(512)S(1)}, f32[512]{0:T(512)}, u32[]{:S(2)}) copy-start(f32[512]{0:T(512)} %copy-done.76) | copy-start | bytes 6148
  609.5 8.0 %copy-start.89 = (f32[1024]{0:T(1024)S(1)}, f32[1024]{0:T(1024)}, u32[]{:S(2)}) copy-start(f32[1024]{0:T(1024)} %param.41) | copy-start | bytes 12292
  617.5 13.1 %copy-start.35 = (f32[512,256]{1,0:T(8,128)S(1)}, f32[512,256]{1,0:T(8,128)}, u32[]{:S(2)}) copy-start(f32[512,256]{1,0:T(8,128)} %copy-done.34) | copy-start | bytes 1572868
  626.2 9.6 %collective-permute-start.9 = (bf16[512,256]{1,0:T(8,128)(2,1)S(1)}, bf16[512,256]{1,0:T(8,128)(2,1)S(1)}, u32[]{:S(2)}, u32[]{:S(2)}) collective-permute-start(bf16[512,256]{1,0:T(8,128)(2,1)S(1)} %reduce_sum.291), channel_id=1, source_target_pairs={{0,1},{1,0},{2,3},{3,2},{4,5},{5,4},{6,7},{7,6},{8,9},{9,8},{10,11... | collective-permute-start | bytes 786440 | tf_op jit(solution)/shard_map/ppermute | solution.py:102
  627.2 9.4 %collective-permute-start.10 = (bf16[512,256]{1,0:T(8,128)(2,1)S(1)}, bf16[512,256]{1,0:T(8,128)(2,1)S(1)}, u32[]{:S(2)}, u32[]{:S(2)}) collective-permute-start(bf16[512,256]{1,0:T(8,128)(2,1)S(1)} %reduce_sum.291), channel_id=1, source_target_pairs={{0,2},{1,3},{2,0},{3,1},{4,6},{5,7},{6,4},{7,5},{8,10},{9,11},{10,... | collective-permute-start | bytes 786440 | tf_op jit(solution)/shard_map/ppermute | solution.py:102
  627.3 15.1 %collective-permute-start.11 = (bf16[512,256]{1,0:T(8,128)(2,1)S(1)}, bf16[512,256]{1,0:T(8,128)(2,1)S(1)}, u32[]{:S(2)}, u32[]{:S(2)}) collective-permute-start(bf16[512,256]{1,0:T(8,128)(2,1)S(1)} %reduce_sum.291), channel_id=1, source_target_pairs={{0,3},{1,2},{2,1},{3,0},{4,7},{5,6},{6,5},{7,4},{8,11},{9,10},{10,... | collective-permute-start | bytes 786440 | tf_op jit(solution)/shard_map/ppermute | solution.py:102
  652.9 26.6 %all-to-all-start.10 = ((bf16[32,32,513]{2,1,0:T(8,128)(2,1)}), bf16[32,32,513]{2,1,0:T(8,128)(2,1)}, u32[]{:S(2)}, u32[]{:S(2)}) async-start(bf16[32,32,513]{2,1,0:T(8,128)(2,1)} %pad_maximum_fusion.3), calls=%async_computation.10 | async-start | bytes 2621440 | tf_op jit(solution)/shard_map/all_to_all | solution.py:113
  663.9 18.9 %copy-start.1 = (bf16[256,1024]{1,0:T(8,128)(2,1)S(1)}, bf16[256,1024]{1,0:T(8,128)(2,1)}, u32[]{:S(2)}) copy-start(bf16[256,1024]{1,0:T(8,128)(2,1)} %param.45) | copy-start | bytes 1572868
  (52 other events, 114.6 us)
Sparse Core Ops, SparseCore 0:
  30.6 43.2 all-gather.1
  375.4 33.2 reduce-scatter.4
  556.0 44.5 reduce-scatter.6

commit v2 on v1

--- a/solution.py
+++ b/solution.py
@@ -1,6 +1,8 @@
 import jax
 import jax.numpy as jnp
 from jax import lax
+from jax.experimental import pallas as pl
+from jax.experimental.pallas import tpu as pltpu
 from jax.sharding import PartitionSpec as P
 
 HEAD_DIM = 64
@@ -192,6 +194,219 @@
     return lax.dot_general(
         left_side, right_side, (((1,), (1,)), ((), ())), preferred_element_type=jnp.float32
     )
+
+
+def padded_columns(rows_t, out_ref):
+    zero = jnp.zeros((HEAD_DIM, rows_t.shape[1]), out_ref.dtype)
+    for h in range(4):
+        mine = rows_t[h * HEAD_DIM : (h + 1) * HEAD_DIM].astype(out_ref.dtype)
+        at = (h // 2) * HEAD_DIM
+        out_ref[h, pl.ds(at, HEAD_DIM), :] = mine
+        out_ref[h, pl.ds(HEAD_DIM - at, HEAD_DIM), :] = zero
+
+
+def padded_rows(rows, out_ref):
+    n = rows.shape[0]
+    lane = lax.broadcasted_iota(jnp.int32, (n, 128), 1)
+    for h in range(4):
+        pair = rows[:, (h // 2) * 128 : (h // 2) * 128 + 128].astype(jnp.float32)
+        if h % 2 != h // 2:
+            pair = pltpu.roll(pair, HEAD_DIM, 1)
+        own = (lane < HEAD_DIM) if h // 2 == 0 else (lane >= HEAD_DIM)
+        out_ref[pl.ds(h * n, n), :] = jnp.where(own, pair, 0.0).astype(out_ref.dtype)
+
+
+def attend_kernel(reach_ref, q_ref, own_ref, prev_ref, att_ref, out_t_ref, lse_ref, qpad_ref, max_ref, sum_ref):
+    q_t = jnp.transpose(q_ref[...].astype(jnp.float32) * score_mult)
+    padded_columns(q_t, qpad_ref)
+    half = BLOCK // 2
+
+    def block(key_rows, value_rows, first):
+        for h in range(4):
+            group = (h // 2) * HEAD_DIM
+            for t in range(2):
+                cols = slice(t * half, (t + 1) * half)
+                rows = half if first and t == 0 else BLOCK
+                scores = jnp.dot(
+                    key_rows[:rows], qpad_ref[h, :, cols], preferred_element_type=jnp.float32
+                )
+                if first:
+                    key_at = lax.broadcasted_iota(jnp.int32, scores.shape, 0)
+                    query_at = lax.broadcasted_iota(jnp.int32, scores.shape, 1) + t * half
+                    scores = jnp.where(key_at > query_at, masked_score, scores)
+                new_max = jnp.max(scores, axis=0, keepdims=True)
+                if not first:
+                    old_max = max_ref[h : h + 1, cols]
+                    new_max = jnp.maximum(new_max, old_max)
+                    shrink = jnp.exp(old_max - new_max)
+                weights = jnp.exp(scores - new_max)
+                total = jnp.sum(weights, axis=0, keepdims=True)
+                part = lax.dot_general(
+                    value_rows[:rows],
+                    weights.astype(jnp.bfloat16),
+                    (((0,), (0,)), ((), ())),
+                    preferred_element_type=jnp.float32,
+                )[group : group + HEAD_DIM]
+                mine = pl.ds(h * HEAD_DIM, HEAD_DIM)
+                if not first:
+                    total = total + sum_ref[h : h + 1, cols] * shrink
+                    part = part + out_t_ref[mine, cols] * shrink
+                max_ref[h : h + 1, cols] = new_max
+                sum_ref[h : h + 1, cols] = total
+                out_t_ref[mine, cols] = part
+
+    block(own_ref[:, :128], own_ref[:, 128:], True)
+
+    @pl.loop(1, reach_ref[0] + 1)
+    def _(step):
+        rows = prev_ref[:, pl.ds(step - 1, 1)].reshape(BLOCK, 256)
+        block(rows[:, :128], rows[:, 128:], False)
+
+    lse_ref[...] = jnp.zeros_like(lse_ref)
+    lse_ref[0:4, :] = max_ref[0:4, :] + jnp.log(sum_ref[0:4, :])
+    for h in range(4):
+        mine = pl.ds(h * HEAD_DIM, HEAD_DIM)
+        out_t_ref[mine, :] = out_t_ref[mine, :] / sum_ref[h : h + 1, :]
+    att_ref[...] = jnp.transpose(out_t_ref[...]).astype(jnp.bfloat16)
+
+
+def attend(reach, queries, own_kv, earlier):
+    vmem = pl.BlockSpec(memory_space=pltpu.VMEM)
+    return pl.pallas_call(
+        attend_kernel,
+        name="attend",
+        in_specs=[pl.BlockSpec(memory_space=pltpu.SMEM), vmem, vmem, vmem],
+        out_specs=[vmem] * 3,
+        out_shape=(
+            jax.ShapeDtypeStruct((BLOCK, 256), jnp.bfloat16),
+            jax.ShapeDtypeStruct((256, BLOCK), jnp.float32),
+            jax.ShapeDtypeStruct((8, BLOCK), jnp.float32),
+        ),
+        scratch_shapes=[
+            pltpu.VMEM((4, 128, BLOCK), jnp.bfloat16),
+            pltpu.VMEM((8, BLOCK), jnp.float32),
+            pltpu.VMEM((8, BLOCK), jnp.float32),
+        ],
+        compiler_params=pltpu.CompilerParams(vmem_limit_bytes=40 << 20),
+        cost_estimate=pl.CostEstimate(
+            flops=5_000_000_000, bytes_accessed=3_000_000, transcendentals=3_000_000
+        ),
+    )(reach, queries, own_kv, earlier)
+
+
+def rotated_back(rows, cosine, signed_sine):
+    lane = lax.broadcasted_iota(jnp.int32, (rows.shape[0], 128), 1)
+    front = (lane % HEAD_DIM) < HEAD_DIM // 2
+    done = []
+    for at in range(0, rows.shape[1], 128):
+        chunk = rows[:, at : at + 128]
+        partner = jnp.where(front, pltpu.roll(chunk, 96, 1), pltpu.roll(chunk, 32, 1))
+        done.append(chunk * cosine - partner * signed_sine)
+    return done
+
+
+def attend_back_kernel(
+    reach_ref, q_ref, own_ref, prev_ref, grad_ref, grad_t_ref, out_t_ref, lse_ref, cos_ref, sin_ref,
+    qgrad_ref, own_grad_ref, prev_grad_ref,
+    qpad_ref, gpad_ref, qrows_ref, grows_ref, ds_ref, p_ref, delta_ref, dq_ref,
+):
+    half = BLOCK // 2
+    q_scaled = q_ref[...].astype(jnp.float32) * score_mult
+    padded_columns(jnp.transpose(q_scaled), qpad_ref)
+    padded_rows(q_scaled, qrows_ref)
+    padded_columns(grad_t_ref[...], gpad_ref)
+    padded_rows(grad_ref[...], grows_ref)
+    both = grad_t_ref[...].astype(jnp.float32) * out_t_ref[...]
+    for h in range(4):
+        delta_ref[h : h + 1, :] = jnp.sum(
+            both[h * HEAD_DIM : (h + 1) * HEAD_DIM], axis=0, keepdims=True
+        )
+
+    def block(key_rows, value_rows, first):
+        for h in range(4):
+            for t in range(2):
+                cols = slice(t * half, (t + 1) * half)
+                wide = slice(h * BLOCK + t * half, h * BLOCK + (t + 1) * half)
+                rows = half if first and t == 0 else BLOCK
+                scores = jnp.dot(
+                    key_rows[:rows], qpad_ref[h, :, cols], preferred_element_type=jnp.float32
+                )
+                weights = jnp.exp(scores - lse_ref[h : h + 1, cols])
+                if first:
+                    key_at = lax.broadcasted_iota(jnp.int32, scores.shape, 0)
+                    query_at = lax.broadcasted_iota(jnp.int32, scores.shape, 1) + t * half
+                    weights = jnp.where(key_at > query_at, 0.0, weights)
+                weight_grad = jnp.dot(
+                    value_rows[:rows], gpad_ref[h, :, cols], preferred_element_type=jnp.float32
+                )
+                score_grad = weights * (weight_grad - delta_ref[h : h + 1, cols])
+                p_ref[:rows, wide] = weights.astype(jnp.bfloat16)
+                ds_ref[:rows, wide] = score_grad.astype(jnp.bfloat16)
+                if rows < BLOCK:
+                    p_ref[rows:, wide] = jnp.zeros((BLOCK - rows, half), jnp.bfloat16)
+                    ds_ref[rows:, wide] = jnp.zeros((BLOCK - rows, half), jnp.bfloat16)
+        key_grad = jnp.dot(ds_ref[...], qrows_ref[...], preferred_element_type=jnp.float32)
+        value_grad = jnp.dot(p_ref[...], grows_ref[...], preferred_element_type=jnp.float32)
+        for h in range(4):
+            group = (h // 2) * HEAD_DIM
+            mine = pl.ds(h * HEAD_DIM, HEAD_DIM)
+            part = lax.dot_general(
+                key_rows,
+                ds_ref[:, h * BLOCK : (h + 1) * BLOCK],
+                (((0,), (0,)), ((), ())),
+                preferred_element_type=jnp.float32,
+            )[group : group + HEAD_DIM]
+            if first:
+                dq_ref[mine, :] = part
+            else:
+                dq_ref[mine, :] = dq_ref[mine, :] + part
+        return key_grad, value_grad
+
+    key_grad, value_grad = block(own_ref[:, :128], own_ref[:, 128:], True)
+    own_grad_ref[:, :128] = key_grad
+    own_grad_ref[:, 128:] = value_grad
+
+    @pl.loop(1, reach_ref[0] + 1)
+    def _(step):
+        rows = prev_ref[:, pl.ds(step - 1, 1)].reshape(BLOCK, 256)
+        key_grad, value_grad = block(rows[:, :128], rows[:, 128:], False)
+        parts = prev_grad_ref.shape[0]
+        shape = (parts, 1, BLOCK // parts, 128)
+        prev_grad_ref[:, pl.ds(step - 1, 1), :, 0:128] = key_grad.astype(jnp.bfloat16).reshape(shape)
+        prev_grad_ref[:, pl.ds(step - 1, 1), :, 128:256] = value_grad.astype(jnp.bfloat16).reshape(shape)
+
+    turned = rotated_back(jnp.transpose(dq_ref[...]) * score_mult, cos_ref[...], sin_ref[...])
+    for i, chunk in enumerate(turned):
+        qgrad_ref[:, i * 128 : (i + 1) * 128] = chunk.astype(jnp.bfloat16)
+
+
+def attend_back(reach, queries, own_kv, earlier, grad, grad_t, out_t, lse, cosine, signed_sine):
+    vmem = pl.BlockSpec(memory_space=pltpu.VMEM)
+    return pl.pallas_call(
+        attend_back_kernel,
+        name="attend_back",
+        in_specs=[pl.BlockSpec(memory_space=pltpu.SMEM)] + [vmem] * 9,
+        out_specs=[vmem] * 3,
+        out_shape=(
+            jax.ShapeDtypeStruct((BLOCK, 256), jnp.bfloat16),
+            jax.ShapeDtypeStruct((BLOCK, 256), jnp.float32),
+            jax.ShapeDtypeStruct(earlier.shape, jnp.bfloat16),
+        ),
+        scratch_shapes=[
+            pltpu.VMEM((4, 128, BLOCK), jnp.bfloat16),
+            pltpu.VMEM((4, 128, BLOCK), jnp.bfloat16),
+            pltpu.VMEM((4 * BLOCK, 128), jnp.bfloat16),
+            pltpu.VMEM((4 * BLOCK, 128), jnp.bfloat16),
+            pltpu.VMEM((BLOCK, 4 * BLOCK), jnp.bfloat16),
+            pltpu.VMEM((BLOCK, 4 * BLOCK), jnp.bfloat16),
+            pltpu.VMEM((8, BLOCK), jnp.float32),
+            pltpu.VMEM((256, BLOCK), jnp.float32),
+        ],
+        compiler_params=pltpu.CompilerParams(vmem_limit_bytes=48 << 20),
+        cost_estimate=pl.CostEstimate(
+            flops=12_000_000_000, bytes_accessed=5_000_000, transcendentals=3_000_000
+        ),
+    )(reach, queries, own_kv, earlier, grad, grad_t, out_t, lse, cosine, signed_sine)
 
 
 def expert_back(grouped_in, grouped_grad, gate_pre, up_pre, gate_mat, up_mat, down_mat):
@@ -286,90 +501,9 @@
     earlier = lax.all_to_all(
         picked_kv.reshape(dp_count, (window - 1) * piece, kv_width), "dp", 0, 0, tiled=True
     )
-    earlier = jnp.moveaxis(earlier.reshape(dp_count, window - 1, piece, kv_width), 1, 0)
-    kv_window = jnp.concatenate(
-        [key_value[None], earlier.reshape(window - 1, BLOCK, kv_width)], axis=0
-    )
-    keys_window = kv_window[:, :, : key_rows.shape[1]]
-    values_window = kv_window[:, :, key_rows.shape[1] :]
-
-    def key_block(packed_query, key_step):
-        return (
-            lax.dynamic_index_in_dim(keys_window, key_step, 0, False),
-            lax.dynamic_index_in_dim(values_window, key_step, 0, False),
-            key_step,
-        )
-
-    def block_scores(query_block, key_block_rows, key_step):
-        query_heads = query_block.reshape(BLOCK, kv_here, head_group, HEAD_DIM)
-        key_heads = key_block_rows.reshape(BLOCK, kv_here, HEAD_DIM)
-        raw_scores = (
-            jnp.einsum("qhgd,khd->hgqk", query_heads, key_heads, preferred_element_type=jnp.float32)
-            * score_mult
-        )
-        return jnp.where(jnp.logical_and(key_step == 0, later_keys), masked_score, raw_scores)
-
-    local_block = 0
-    packed_query = my_blocks[local_block]
-    block_reach = my_offsets[local_block]
-    query_block = queries
-
-    def max_step(
-        key_step,
-        max_state,
-        packed_query=packed_query,
-        block_reach=block_reach,
-        query_block=query_block,
-    ):
-
-        def max_live(running):
-            running_max, running_sum = running
-            key_part, value_part, row_start = key_block(packed_query, key_step)
-            scores = block_scores(query_block, key_part, key_step)
-            new_max = jnp.maximum(running_max, jnp.max(scores, axis=-1))
-            new_sum = running_sum * jnp.exp(running_max - new_max) + jnp.sum(
-                jnp.exp(scores - new_max[..., None]), axis=-1
-            )
-            return (new_max, new_sum)
-
-        return lax.cond(key_step <= block_reach, max_live, lambda running: running, max_state)
-
-    start_state = (
-        jnp.full((kv_here, head_group, BLOCK), masked_score, jnp.float32),
-        jnp.zeros((kv_here, head_group, BLOCK), jnp.float32),
-    )
-    running_max, running_sum = lax.fori_loop(0, window, max_step, start_state)
-    block_lse = running_max + jnp.log(running_sum)
-
-    def sum_step(
-        key_step,
-        accumulated,
-        packed_query=packed_query,
-        block_reach=block_reach,
-        query_block=query_block,
-        block_lse=block_lse,
-    ):
-
-        def sum_live(running_total):
-            key_part, value_part, row_start = key_block(packed_query, key_step)
-            prob_block = jnp.exp(
-                block_scores(query_block, key_part, key_step) - block_lse[..., None]
-            ).astype(jnp.bfloat16)
-            value_heads = value_part.reshape(BLOCK, kv_here, HEAD_DIM)
-            return running_total + jnp.einsum(
-                "hgqk,khd->qhgd", prob_block, value_heads, preferred_element_type=jnp.float32
-            )
-
-        return lax.cond(
-            key_step <= block_reach, sum_live, lambda running_total: running_total, accumulated
-        )
-
-    block_out = lax.fori_loop(
-        0, window, sum_step, jnp.zeros((BLOCK, kv_here, head_group, HEAD_DIM), jnp.float32)
-    )
-    attended_blocks = block_out.reshape(BLOCK, kv_here * head_group * HEAD_DIM)
-    lse_blocks = [block_lse]
-    attended = attended_blocks.astype(jnp.bfloat16)
+    earlier = earlier.reshape(dp_count, window - 1, piece, kv_width)
+    reach = my_offsets
+    attended, attended_t, block_lse = attend(reach, queries, key_value, earlier)
     branch_part = jnp.dot(attended, w_out, preferred_element_type=jnp.float32)
     branch_sent = jnp.moveaxis(
         branch_part.astype(jnp.bfloat16).reshape(tokens_here, mp_count, column_share), 1, 0
@@ -495,115 +629,22 @@
     branch_grad = (residual_mult * residual_grad).astype(jnp.bfloat16)
     out_weight_grad = row_contract(attended, branch_grad)
     attended_grad = times_transposed(branch_grad, w_out).astype(jnp.bfloat16)
-    key_grad_all = jnp.zeros((window, BLOCK, kv_here * HEAD_DIM), jnp.float32)
-    value_grad_all = jnp.zeros((window, BLOCK, kv_here * HEAD_DIM), jnp.float32)
-    local_block = 0
-    packed_query = my_blocks[local_block]
-    block_reach = my_offsets[local_block]
-    query_block = queries
-    block_lse = lse_blocks[local_block]
-    grad_heads = attended_grad.reshape(BLOCK, kv_here, head_group, HEAD_DIM)
-
-    def delta_step(
-        key_step,
-        accumulated,
-        packed_query=packed_query,
-        block_reach=block_reach,
-        query_block=query_block,
-        block_lse=block_lse,
-        grad_heads=grad_heads,
-    ):
-
-        def delta_live(running_total):
-            key_part, value_part, row_start = key_block(packed_query, key_step)
-            prob_block = jnp.exp(
-                block_scores(query_block, key_part, key_step) - block_lse[..., None]
-            )
-            value_heads = value_part.reshape(BLOCK, kv_here, HEAD_DIM)
-            prob_grad = jnp.einsum(
-                "qhgd,khd->hgqk", grad_heads, value_heads, preferred_element_type=jnp.float32
-            )
-            return running_total + jnp.sum(prob_block * prob_grad, axis=-1)
-
-        return lax.cond(
-            key_step <= block_reach, delta_live, lambda running_total: running_total, accumulated
-        )
-
-    delta_sum = lax.fori_loop(
-        0, window, delta_step, jnp.zeros((kv_here, head_group, BLOCK), jnp.float32)
-    )
-
-    def grad_step(
-        key_step,
-        grad_carry,
-        packed_query=packed_query,
-        block_reach=block_reach,
-        query_block=query_block,
-        block_lse=block_lse,
-        grad_heads=grad_heads,
-        delta_sum=delta_sum,
-    ):
-        query_acc, key_acc, value_acc = grad_carry
-        key_part, value_part, row_start = key_block(packed_query, key_step)
-
-        def grad_live(unused):
-            prob_block = jnp.exp(
-                block_scores(query_block, key_part, key_step) - block_lse[..., None]
-            )
-            query_heads = query_block.reshape(BLOCK, kv_here, head_group, HEAD_DIM)
-            key_heads = key_part.reshape(BLOCK, kv_here, HEAD_DIM)
-            value_heads = value_part.reshape(BLOCK, kv_here, HEAD_DIM)
-            prob_grad = jnp.einsum(
-                "qhgd,khd->hgqk", grad_heads, value_heads, preferred_element_type=jnp.float32
-            )
-            score_grad = (prob_block * (prob_grad - delta_sum[..., None])).astype(jnp.bfloat16)
-            query_add = (
-                jnp.einsum(
-                    "hgqk,khd->qhgd", score_grad, key_heads, preferred_element_type=jnp.float32
-                )
-                * score_mult
-            )
-            key_add = (
-                jnp.einsum(
-                    "hgqk,qhgd->khd", score_grad, query_heads, preferred_element_type=jnp.float32
-                )
-                * score_mult
-            )
-            value_add = jnp.einsum(
-                "hgqk,qhgd->khd",
-                prob_block.astype(jnp.bfloat16),
-                grad_heads,
-                preferred_element_type=jnp.float32,
-            )
-            return (
-                query_add,
-                key_add.reshape(BLOCK, kv_here * HEAD_DIM),
-                value_add.reshape(BLOCK, kv_here * HEAD_DIM),
-            )
-
-        def dead(unused):
-            return (
-                jnp.zeros((BLOCK, kv_here, head_group, HEAD_DIM), jnp.float32),
-                jnp.zeros((BLOCK, kv_here * HEAD_DIM), jnp.float32),
-                jnp.zeros((BLOCK, kv_here * HEAD_DIM), jnp.float32),
-            )
-
-        query_add, key_add, value_add = lax.cond(key_step <= block_reach, grad_live, dead, 0)
-        key_acc = lax.dynamic_update_index_in_dim(key_acc, key_add, row_start, 0)
-        value_acc = lax.dynamic_update_index_in_dim(value_acc, value_add, row_start, 0)
-        return (query_acc + query_add, key_acc, value_acc)
-
-    start_grads = (
-        jnp.zeros((BLOCK, kv_here, head_group, HEAD_DIM), jnp.float32),
-        key_grad_all,
-        value_grad_all,
-    )
-    query_acc, key_grad_all, value_grad_all = lax.fori_loop(0, window, grad_step, start_grads)
-    query_grad_blocks = query_acc.reshape(BLOCK, kv_here * head_group * HEAD_DIM)
-    kv_grads = jnp.concatenate([key_grad_all, value_grad_all], axis=2)
-    later_grads = kv_grads[1:].astype(jnp.bfloat16)
-    later_grads = later_grads.reshape(window - 1, dp_count, piece, kv_width)
-    later_grads = jnp.moveaxis(later_grads, 1, 0).reshape(dp_count, -1, kv_width)
+    attended_grad_t = times_transposed(w_out, branch_grad).astype(jnp.bfloat16)
+    cosine_wide = jnp.tile(cosine, (1, 4))
+    sine_wide = jnp.tile(jnp.concatenate([-sine_table, sine_table], axis=1), (1, 2))
+    query_pre_grad, own_grads, later_grads = attend_back(
+        reach,
+        queries,
+        key_value,
+        earlier,
+        attended_grad,
+        attended_grad_t,
+        attended_t,
+        block_lse,
+        cosine_wide,
+        sine_wide,
+    )
+    later_grads = later_grads.reshape(dp_count, -1, kv_width)
     gathered_grads = lax.all_to_all(later_grads, "dp", 0, 0, tiled=True)
     after = block_order[:, None] + back_steps[None, :]
     after_hit = after[:, :, None] == block_ids[None, None, :]
@@ -618,10 +659,9 @@
         jnp.where(after_live[:, :, None, None], taken.astype(jnp.float32), 0.0), axis=1
     )
     home = lax.all_to_all(summed.astype(jnp.bfloat16), "dp", 0, 0, tiled=True)
-    kv_grad_sum = kv_grads[0] + home.reshape(BLOCK, kv_width).astype(jnp.float32)
+    kv_grad_sum = own_grads + home.reshape(BLOCK, kv_width).astype(jnp.float32)
     key_grad_sum = kv_grad_sum[:, : key_rows.shape[1]]
     value_grad_sum = kv_grad_sum[:, key_rows.shape[1] :]
-    query_pre_grad = rotate_back(query_grad_blocks, cosine, sine_table).astype(jnp.bfloat16)
     key_pre_grad = rotate_back(key_grad_sum, cosine, sine_table).astype(jnp.bfloat16)
     value_pre_grad = value_grad_sum.astype(jnp.bfloat16)
     normed_part = (

time: 702 us -> 590 us (0.84)
  starting transfers between devices: 138 us -> 85.1 us
  local copies, waits for them, and re-layouts: 160 us -> 132 us
  blocking collectives: 102 us -> 79.9 us
  matrix products: 64.3 us -> 43.3 us
  Pallas kernels: 0 us -> 15.4 us
  waiting for transfers between devices: 126 us -> 140 us
  loops' own time: 11.5 us -> 0 us
    all_to_all x1, starting transfers between devices: 63.9 us -> 6.9 us  [per_device(): gathered_grads = lax.all_to_all(later_grads, 'dp', 0, 0, tiled=True)]
    all_to_all x1, blocking collectives: 64.6 us -> 42.2 us  [per_device(): lax.all_to_all(outgoing, 'dp', split_axis=0, concat_axis=0, tiled=True)]
    dot_general x9 -> x0, matrix products: 20.2 us -> none  [the longest x3 6.31 us: block_scores(): jnp.einsum('qhgd,khd->hgqk', query_heads, key_heads, preferred_element_ty...]
    pallas_call x0 -> x2, Pallas kernels: none -> 15.4 us  [the longest x1 7.98 us: attend_back(): pl.pallas_call(attend_back_kernel, name='attend_back', in_specs=[pl.Block...]
    another operation x20 -> x0, loops' own time: 11.5 us -> none  [the longest x1 2.83 us: per_device(): lax.fori_loop(0, window, grad_step, start_grads)]
    dynamic_update_slice x12 -> x0, local copies, waits for them, and re-layouts: 8.15 us -> none  [the longest x8 7.65 us: grad_step(): lax.dynamic_update_index_in_dim(value_acc, value_add, row_start, 0)]
    all_to_all x4, waiting for transfers between devices: 27.3 us -> 35 us  [reduced_share(): parts = lax.all_to_all(x, axis, 0, 0, tiled=True)]
    unnamed x179 -> x152, local copies, waits for them, and re-layouts: 24.8 us -> 21.5 us
  transfers between devices with their start and end apart: 25 -> 25, of which waited for: 17 -> 16; matrix products, arithmetic and copies ran while one was open for 31% -> 28% of each run, Pallas kernels for 0% -> 3%
where the time goes in v2:
time: 590 us; the launch traced here: 579 us
  waiting for transfers between devices  140 us (24%)
  local copies, waits for them, and re-layouts  132 us (22%)
  starting transfers between devices  85.1 us (14%)
  blocking collectives  79.9 us (14%)
  other arithmetic  66.8 us (11%)
  matrix products  43.3 us (7%)
  between operations  16.2 us (3%)
  Pallas kernels  15.4 us (3%)
    all_to_all x2, waiting for transfers between devices, exchange_both(): parts = lax.all_to_all(parts, axis, split_axis=0, concat_axis=0, tiled=True)  49.5 us
    all_to_all x1, blocking collectives, per_device(): lax.all_to_all(outgoing, 'dp', split_axis=0, concat_axis=0, tiled=True)  42.2 us
    all_to_all x1, blocking collectives, per_device(): lax.all_to_all(outgoing_grad, 'dp', split_axis=0, concat_axis=0, tiled=True)  37.7 us
    all_to_all x4, waiting for transfers between devices, reduced_share(): parts = lax.all_to_all(x, axis, 0, 0, tiled=True)  35 us
    ppermute x12, waiting for transfers between devices, from_peers(): got.append(lax.ppermute(x, axis, [(i, i ^ flip) for i in range(4)]))  28.7 us
    all_to_all x4, starting transfers between devices, reduced_share(): parts = lax.all_to_all(x, axis, 0, 0, tiled=True)  22.5 us
    unnamed x152, local copies, waits for them, and re-layouts  21.5 us
    all_to_all x1, waiting for transfers between devices, per_device(): lax.all_to_all(picked_kv.reshape(dp_count, (window - 1) * piece, kv_width...  20 us
  transfers between devices with their start and end apart: 25, of which 16 were waited for; matrix products, arithmetic and copies ran while one was open for 28% of the time, Pallas kernels for 3%

profile of v2, /device:TPU:1, one launch (start us, length us, event | category | flops | bytes accessed | tf_op | source)
XLA Modules:
  0.0 579.0 jit_solution(4064958918539900558)
XLA Ops:
  10.2 1.8 iota_subtract_fusion
  15.8 1.9 fusion.55
  19.2 9.8 %all-to-all-start = ((bf16[32,16,256]{2,1,0:T(8,128)(2,1)}), bf16[32,16,256]{2,1,0:T(8,128)(2,1)S(1)}, u32[]{:S(2)}, u32[]{:S(2)}) async-start(bf16[32,16,256]{2,1,0:T(8,128)(2,1)} %bitcast.8), calls=%async_computation | async-start | bytes 524288 | tf_op jit(solution)/shard_map/all_to_all | solution.py:492
  35.2 2.4 all-to-all-done
  39.4 5.4 all-to-all-start.1
  47.5 20.0 %all-to-all-done.1 = bf16[32,48,256]{2,1,0:T(8,128)(2,1)S(1)} async-done(((bf16[32,48,256]{2,1,0:T(8,128)(2,1)}), bf16[32,48,256]{2,1,0:T(8,128)(2,1)S(1)}, u32[]{:S(2)}, u32[]{:S(2)}) %all-to-all-start.1) | async-done | bytes 786464 | tf_op jit(solution)/shard_map/all_to_all | solution.py:501
  67.5 7.4 %attend.1 = (bf16[512,256]{1,0:T(8,128)(2,1)S(1)}, f32[256,512]{1,0:T(8,128)S(1)}, f32[8,512]{1,0:T(8,128)S(1)}) custom-call(s32[1]{0:T(128)} %bitcast.2.reach_ref, bf16[512,256]{1,0:T(8,128)(2,1)S(1)} %copy.110.q_ref, bf16[512,256]{1,0:T(8,128)(2,1)} %pad_maximum_fusion.10.own_ref, bf16[32,3,16,256]{3,2,1,0:T(8,128)(2,1)S(1)} %bitcast.279), custom_call_target="tpu_custom_call" | custom-call | flops 5000000000 | bytes 3000000 | tf_op jit(solution)/shard_map/attend/pallas_call | solution.py:275
  76.5 7.1 %all-to-all-start.2 = ((bf16[4,512,256]{2,1,0:T(8,128)(2,1)}), bf16[4,512,256]{2,1,0:T(8,128)(2,1)}, u32[]{:S(2)}, u32[]{:S(2)}) async-start(bf16[4,512,256]{2,1,0:T(8,128)(2,1)} %bitcast.292), calls=%async_computation.2 | async-start | bytes 2097152 | tf_op jit(solution)/shard_map/all_to_all | solution.py:115
  84.5 15.5 %scatter_custom_fusion = s32[5120]{0:T(1024)S(1)} fusion(s32[4096]{0:T(1024)S(1)} %bitcast.327, s32[4096]{0:T(1024)S(1)} %reshape.816, s32[]{:T(128)} %constant.66.clone.1), kind=kCustom, calls=%fused_computation.162 | custom fusion | bytes 20484 | tf_op jit(solution)/shard_map/scatter | solution.py:528
  103.3 3.2 collective-permute-start.1
  108.8 3.9 collective-permute-done.1
  112.7 6.0 %collective-permute-done.2 = bf16[512,256]{1,0:T(8,128)(2,1)S(1)} collective-permute-done((bf16[512,256]{1,0:T(8,128)(2,1)S(1)}, bf16[512,256]{1,0:T(8,128)(2,1)S(1)}, u32[]{:S(2)}, u32[]{:S(2)}) %collective-permute-start.2) | collective-permute-done | bytes 262176 | tf_op jit(solution)/shard_map/ppermute | solution.py:104
  119.8 2.9 gather_fusion.2
  127.6 5.1 gather_fusion.3
  132.6 2.1 broadcast_select_fusion
  134.7 42.2 %all_to_all.60 = bf16[32,40,1024]{2,1,0:T(8,128)(2,1)} all-to-all(bf16[32,40,1024]{2,1,0:T(8,128)(2,1)S(1)} %bitcast.284), channel_id=1, replica_groups=mesh['dp'=32,'mp'=4] {'dp'}, dimensions={0} | all-to-all | bytes 5242880 | tf_op jit(solution)/shard_map/all_to_all | solution.py:545
  176.9 3.7 fusion.28
  185.9 1.8 copy.120
  187.7 8.7 %all-to-all-start.4 = ((bf16[128,1,40,256]{3,2,1,0:T(8,128)(2,1)}), bf16[128,1,40,256]{3,2,1,0:T(8,128)(2,1)}, u32[]{:S(2)}, u32[]{:S(2)}) async-start(bf16[128,1,40,256]{3,2,1,0:T(8,128)(2,1)} %bitcast.282), calls=%async_computation.4 | async-start | bytes 5242880 | tf_op jit(solution)/shard_map/all_to_all | solution.py:64
  198.3 5.1 gather_fusion.5
  206.3 25.5 %all-to-all-done.4 = bf16[128,1,40,256]{3,2,1,0:T(8,128)(2,1)} async-done(((bf16[128,1,40,256]{3,2,1,0:T(8,128)(2,1)}), bf16[128,1,40,256]{3,2,1,0:T(8,128)(2,1)}, u32[]{:S(2)}, u32[]{:S(2)}) %all-to-all-start.4) | async-done | bytes 2621472 | tf_op jit(solution)/shard_map/all_to_all | solution.py:64
  231.8 18.0 %gather_fusion.4 = bf16[4096,256]{1,0:T(8,128)(2,1)} fusion(bf16[5120,256]{1,0:T(8,128)(2,1)} %bitcast.51, s32[4096]{0:T(1024)S(1)} %fusion.39), kind=kCustom, calls=%fused_computation.2.clone | custom fusion | bytes 4210688 | tf_op jit(solution)/shard_map/jit(_take)/gather | solution.py:599
  249.8 2.6 fusion.2
  254.9 2.1 collective-permute-start.8
  257.8 1.7 collective-permute-done.8
  260.4 15.7 %scatter_custom_fusion.1 = f32[5120]{0:T(1024)S(1)} fusion(s32[4096]{0:T(1024)} %bitcast.328, f32[4096]{0:T(1024)S(1)} %reshape.824, f32[]{:T(128)} %constant.63.clone.1), kind=kCustom, calls=%fused_computation.160 | custom fusion | bytes 20992 | tf_op jit(solution)/shard_map/scatter | solution.py:531
  276.3 2.5 multiply_convert_fusion
  278.8 37.7 %all_to_all.61 = bf16[32,40,1024]{2,1,0:T(8,128)(2,1)S(1)} all-to-all(bf16[32,40,1024]{2,1,0:T(8,128)(2,1)S(1)} %bitcast.283), channel_id=1, replica_groups=mesh['dp'=32,'mp'=4] {'dp'}, dimensions={0} | all-to-all | bytes 5242880 | tf_op jit(solution)/shard_map/all_to_all | solution.py:567
  316.5 2.5 fusion.23
  322.8 1.9 copy.124
  324.7 6.8 %all-to-all-start.6 = ((bf16[128,1,40,256]{3,2,1,0:T(8,128)(2,1)}), bf16[128,1,40,256]{3,2,1,0:T(8,128)(2,1)}, u32[]{:S(2)}, u32[]{:S(2)}) async-start(bf16[128,1,40,256]{3,2,1,0:T(8,128)(2,1)} %bitcast.281), calls=%async_computation.6 | async-start | bytes 5242880 | tf_op jit(solution)/shard_map/all_to_all | solution.py:64
  338.5 4.7 fusion.21
  343.2 24.0 %all-to-all-done.6 = bf16[128,1,40,256]{3,2,1,0:T(8,128)(2,1)} async-done(((bf16[128,1,40,256]{3,2,1,0:T(8,128)(2,1)}), bf16[128,1,40,256]{3,2,1,0:T(8,128)(2,1)}, u32[]{:S(2)}, u32[]{:S(2)}) %all-to-all-start.6) | async-done | bytes 2621472 | tf_op jit(solution)/shard_map/all_to_all | solution.py:64
  367.2 18.0 %gather_fusion.6 = bf16[4096,256]{1,0:T(8,128)(2,1)} fusion(bf16[5120,256]{1,0:T(8,128)(2,1)} %bitcast.76, s32[4096]{0:T(1024)S(1)} %fusion.39), kind=kCustom, calls=%fused_computation.6.clone | custom fusion | bytes 4210688 | tf_op jit(solution)/shard_map/jit(_take)/gather | solution.py:609
  385.2 5.1 bitcast_reduce_fusion
  392.8 1.9 collective-permute-start.5
  394.7 4.3 fusion.19
  399.0 1.8 collective-permute-done.4
  400.8 5.8 %collective-permute-done.5 = bf16[512,256]{1,0:T(8,128)(2,1)S(1)} collective-permute-done((bf16[512,256]{1,0:T(8,128)(2,1)S(1)}, bf16[512,256]{1,0:T(8,128)(2,1)S(1)}, u32[]{:S(2)}, u32[]{:S(2)}) %collective-permute-start.5) | collective-permute-done | bytes 262176 | tf_op jit(solution)/shard_map/ppermute | solution.py:104
  407.7 2.9 gather_fusion.7
  420.3 8.0 %attend_back.1 = (bf16[512,256]{1,0:T(8,128)(2,1)S(1)}, f32[512,256]{1,0:T(8,128)S(1)}, bf16[32,3,16,256]{3,2,1,0:T(8,128)(2,1)}) custom-call(s32[1]{0:T(128)} %bitcast.2.reach_ref, bf16[512,256]{1,0:T(8,128)(2,1)S(1)} %copy.110.q_ref, bf16[512,256]{1,0:T(8,128)(2,1)} %pad_maximum_fusion.10.own_ref, bf16[32,3,16,256]{3,2,1,0:T(8,128)(2,1)S(1)} %bitcast.280, ...), custom_call_target="tpu_custom_call" | custom-call | flops 12000000000 | bytes 5000000 | tf_op jit(solution)/shard_map/attend_back/pallas_call | solution.py:385
  428.3 6.9 %all-to-all-start.7 = ((bf16[32,48,256]{2,1,0:T(8,128)(2,1)}), bf16[32,48,256]{2,1,0:T(8,128)(2,1)S(1)}, u32[]{:S(2)}, u32[]{:S(2)}) async-start(bf16[32,48,256]{2,1,0:T(8,128)(2,1)} %bitcast.87), calls=%async_computation.7 | async-start | bytes 1572864 | tf_op jit(solution)/shard_map/all_to_all | solution.py:648
  435.3 3.7 fusion.20
  440.5 6.3 %copy.153 = bf16[2,1024,512]{1,0,2:T(2,128)(2,1)} copy(bf16[2,1024,512]{2,1,0:T(8,128)(2,1)} %pad_maximum_fusion.2) | data formatting | bytes 4194304
  446.8 3.5 copy.164
  452.0 2.3 select_reduce_fusion
  454.3 7.9 %all-to-all-start.8 = ((bf16[32,16,256]{2,1,0:T(8,128)(2,1)}), bf16[32,16,256]{2,1,0:T(8,128)(2,1)S(1)}, u32[]{:S(2)}, u32[]{:S(2)}) async-start(bf16[32,16,256]{2,1,0:T(8,128)(2,1)} %select_reduce_fusion), calls=%async_computation.8 | async-start | bytes 524288 | tf_op jit(solution)/shard_map/all_to_all | solution.py:661
  462.2 2.2 convolution_convert_fusion.1
  466.0 4.5 all-to-all-done.8
  470.5 3.9 all-to-all-start.11
  478.3 18.5 %all-to-all-done.11 = bf16[32,32,289]{2,1,0:T(8,128)(2,1)S(1)} async-done(((bf16[32,32,289]{2,1,0:T(8,128)(2,1)}), bf16[32,32,289]{2,1,0:T(8,128)(2,1)S(1)}, u32[]{:S(2)}, u32[]{:S(2)}) %all-to-all-start.11) | async-done | bytes 591904 | tf_op jit(solution)/shard_map/all_to_all | solution.py:115
  497.6 7.6 %all-to-all-start.9 = ((bf16[4,512,256]{2,1,0:T(8,128)(2,1)}), bf16[4,512,256]{2,1,0:T(8,128)(2,1)S(1)}, u32[]{:S(2)}, u32[]{:S(2)}) async-start(bf16[4,512,256]{2,1,0:T(8,128)(2,1)} %bitcast.274), calls=%async_computation.9 | async-start | bytes 2097152 | tf_op jit(solution)/shard_map/all_to_all | solution.py:115
  505.3 4.4 fusion.1
  509.7 1.8 add_convert_fusion.2
  511.5 1.9 convert_element_type.309
  515.6 4.7 all-to-all-done.9
  521.7 3.4 collective-permute-start.11
  528.0 2.9 collective-permute-done.10
  530.9 5.8 %collective-permute-done.11 = bf16[512,256]{1,0:T(8,128)(2,1)S(1)} collective-permute-done((bf16[512,256]{1,0:T(8,128)(2,1)S(1)}, bf16[512,256]{1,0:T(8,128)(2,1)S(1)}, u32[]{:S(2)}, u32[]{:S(2)}) %collective-permute-start.11) | collective-permute-done | bytes 262176 | tf_op jit(solution)/shard_map/ppermute | solution.py:104
  536.9 1.7 gather_fusion.8
  540.3 2.0 fusion.18
  544.0 4.0 all-to-all-start.10
  555.7 2.4 dynamic-slice_add_fusion
  558.1 11.9 %all-to-all-done.10 = bf16[32,32,513]{2,1,0:T(8,128)(2,1)S(1)} async-done(((bf16[32,32,513]{2,1,0:T(8,128)(2,1)}), bf16[32,32,513]{2,1,0:T(8,128)(2,1)S(1)}, u32[]{:S(2)}, u32[]{:S(2)}) %all-to-all-start.10) | async-done | bytes 1050656 | tf_op jit(solution)/shard_map/all_to_all | solution.py:115
  (330 shorter events, 99.0 us)
Async XLA Ops:
  7.2 67.8 %copy-start = (bf16[256,1024]{1,0:T(8,128)(2,1)S(1)}, bf16[256,1024]{1,0:T(8,128)(2,1)}, u32[]{:S(2)}) copy-start(bf16[256,1024]{1,0:T(8,128)(2,1)} %param.29) | copy-start | bytes 1572868
  12.6 5.3 copy-start.7
  12.6 5.3 copy-start.41
  12.6 5.3 copy-start.69
  14.9 3.6 copy-start.54
  17.7 11.4 %copy-start.44 = (bf16[1,128,1024]{2,1,0:T(8,128)(2,1)S(1)}, bf16[1,128,1024]{2,1,0:T(8,128)(2,1)}, u32[]{:S(2)}) copy-start(bf16[1,128,1024]{2,1,0:T(8,128)(2,1)} %param.34) | copy-start | bytes 786436
  17.8 11.5 %copy-start.46 = (bf16[1,1024,128]{2,1,0:T(8,128)(2,1)S(1)}, bf16[1,1024,128]{2,1,0:T(8,128)(2,1)}, u32[]{:S(2)}) copy-start(bf16[1,1024,128]{2,1,0:T(8,128)(2,1)} %param.33) | copy-start | bytes 786436
  17.8 11.5 %copy-start.47 = (bf16[1,1024,128]{2,1,0:T(8,128)(2,1)S(1)}, bf16[1,1024,128]{2,1,0:T(8,128)(2,1)}, u32[]{:S(2)}) copy-start(bf16[1,1024,128]{2,1,0:T(8,128)(2,1)} %param.32) | copy-start | bytes 786436
  18.4 14.5 %copy-start.35 = (bf16[1024,256]{1,0:T(8,128)(2,1)S(1)}, bf16[1024,256]{1,0:T(8,128)(2,1)}, u32[]{:S(2)}) copy-start(bf16[1024,256]{1,0:T(8,128)(2,1)} %param.26) | copy-start | bytes 1572868
  19.2 18.4 %all-to-all-start = ((bf16[32,16,256]{2,1,0:T(8,128)(2,1)}), bf16[32,16,256]{2,1,0:T(8,128)(2,1)S(1)}, u32[]{:S(2)}, u32[]{:S(2)}) async-start(bf16[32,16,256]{2,1,0:T(8,128)(2,1)} %bitcast.8), calls=%async_computation | async-start | bytes 524288 | tf_op jit(solution)/shard_map/all_to_all | solution.py:492
  29.0 147.9 %all-gather.2.cloned.1.call-start = ((), (), s32[]{:S(2)}) async-start(), calls=%async_computation.14 | async-start | bytes 3932160 | tf_op jit(solution)/shard_map/all_gather | solution.py:39
  29.2 3.7 copy-start.55
  30.2 4.1 copy-start.38
  39.4 28.1 %all-to-all-start.1 = ((bf16[32,48,256]{2,1,0:T(8,128)(2,1)}), bf16[32,48,256]{2,1,0:T(8,128)(2,1)S(1)}, u32[]{:S(2)}, u32[]{:S(2)}) async-start(bf16[32,48,256]{2,1,0:T(8,128)(2,1)} %bitcast_select_fusion), calls=%async_computation.1 | async-start | bytes 1572864 | tf_op jit(solution)/shard_map/all_to_all | solution.py:501
  46.7 20.8 %copy-start.23 = (s32[512,8]{1,0:T(8,128)}, s32[512,8]{1,0:T(8,128)S(1)}, u32[]{:S(2)}) copy-start(s32[512,8]{1,0:T(8,128)S(1)} %copy.116) | copy-start | bytes 49156
  76.5 25.0 %all-to-all-start.2 = ((bf16[4,512,256]{2,1,0:T(8,128)(2,1)}), bf16[4,512,256]{2,1,0:T(8,128)(2,1)}, u32[]{:S(2)}, u32[]{:S(2)}) async-start(bf16[4,512,256]{2,1,0:T(8,128)(2,1)} %bitcast.292), calls=%async_computation.2 | async-start | bytes 2097152 | tf_op jit(solution)/shard_map/all_to_all | solution.py:115
  84.3 17.2 %copy-start.59 = (s32[4096,1]{0,1:T(1,128)}, s32[4096,1]{0,1:T(1,128)S(1)}, u32[]{:S(2)}) copy-start(s32[4096,1]{0,1:T(1,128)S(1)} %compare_select_fusion) | copy-start | bytes 49156
  103.0 5.8 %collective-permute-start = (bf16[512,256]{1,0:T(8,128)(2,1)S(1)}, bf16[512,256]{1,0:T(8,128)(2,1)S(1)}, u32[]{:S(2)}, u32[]{:S(2)}) collective-permute-start(bf16[512,256]{1,0:T(8,128)(2,1)S(1)} %reduce_sum.261), channel_id=1, source_target_pairs={{0,1},{1,0},{2,3},{3,2},{4,5},{5,4},{6,7},{7,6},{8,9},{9,8},{10,11... | collective-permute-start | bytes 786440 | tf_op jit(solution)/shard_map/ppermute | solution.py:104
  103.3 9.4 %collective-permute-start.1 = (bf16[512,256]{1,0:T(8,128)(2,1)S(1)}, bf16[512,256]{1,0:T(8,128)(2,1)S(1)}, u32[]{:S(2)}, u32[]{:S(2)}) collective-permute-start(bf16[512,256]{1,0:T(8,128)(2,1)S(1)} %reduce_sum.261), channel_id=1, source_target_pairs={{0,2},{1,3},{2,0},{3,1},{4,6},{5,7},{6,4},{7,5},{8,10},{9,11},{10,... | collective-permute-start | bytes 786440 | tf_op jit(solution)/shard_map/ppermute | solution.py:104
  106.5 12.2 %collective-permute-start.2 = (bf16[512,256]{1,0:T(8,128)(2,1)S(1)}, bf16[512,256]{1,0:T(8,128)(2,1)S(1)}, u32[]{:S(2)}, u32[]{:S(2)}) collective-permute-start(bf16[512,256]{1,0:T(8,128)(2,1)S(1)} %reduce_sum.261), channel_id=1, source_target_pairs={{0,3},{1,2},{2,1},{3,0},{4,7},{5,6},{6,5},{7,4},{8,11},{9,10},{10,... | collective-permute-start | bytes 786440 | tf_op jit(solution)/shard_map/ppermute | solution.py:104
  127.5 5.1 copy-start.53
  176.9 3.7 copy-start.22
  176.9 3.8 copy-start.30
  187.7 8.7 %copy-start.24 = (s32[512,8]{1,0:T(8,128)S(1)}, s32[512,8]{1,0:T(8,128)}, u32[]{:S(2)}) copy-start(s32[512,8]{1,0:T(8,128)} %copy-done.23) | copy-start | bytes 49156
  187.7 8.9 %copy-start.12 = (bf16[512,1024]{1,0:T(8,128)(2,1)S(1)}, bf16[512,1024]{1,0:T(8,128)(2,1)}, u32[]{:S(2)}) copy-start(bf16[512,1024]{1,0:T(8,128)(2,1)} %param.35) | copy-start | bytes 3145732
  187.7 44.1 %all-to-all-start.4 = ((bf16[128,1,40,256]{3,2,1,0:T(8,128)(2,1)}), bf16[128,1,40,256]{3,2,1,0:T(8,128)(2,1)}, u32[]{:S(2)}, u32[]{:S(2)}) async-start(bf16[128,1,40,256]{3,2,1,0:T(8,128)(2,1)} %bitcast.282), calls=%async_computation.4 | async-start | bytes 5242880 | tf_op jit(solution)/shard_map/all_to_all | solution.py:64
  198.3 6.2 %copy-start.40 = (bf16[1024,32]{0,1:T(8,128)(2,1)S(1)}, bf16[1024,32]{0,1:T(8,128)(2,1)}, u32[]{:S(2)}) copy-start(bf16[1024,32]{0,1:T(8,128)(2,1)} %param.31) | copy-start | bytes 196612
  204.5 180.7 %copy-start.50 = (pred[4096]{0:T(1024)(128)(4,1)}, pred[4096]{0:T(1024)(128)(4,1)S(1)}, u32[]{:S(2)}) copy-start(pred[4096]{0:T(1024)(128)(4,1)S(1)} %compare_and_fusion) | copy-start | bytes 12292
  252.7 4.3 collective-permute-start.6
  253.7 4.0 collective-permute-start.7
  254.9 4.6 collective-permute-start.8
  260.2 18.6 %copy-start.25 = (f32[512,8]{1,0:T(8,128)}, f32[512,8]{1,0:T(8,128)S(1)}, u32[]{:S(2)}) copy-start(f32[512,8]{1,0:T(8,128)S(1)} %copy.113) | copy-start | bytes 49156
  276.3 40.2 %copy-start.31 = (bf16[512,3072]{0,1:T(8,128)(2,1)S(1)}, bf16[512,3072]{0,1:T(8,128)(2,1)}, u32[]{:S(2)}) copy-start(bf16[512,3072]{0,1:T(8,128)(2,1)} %all-gather.2.cloned.1.call-done) | copy-start | bytes 9437188
  278.8 37.7 %copy-start.19 = (f32[512,32,40]{0,2,1:T(8,128)S(1)}, f32[512,32,40]{0,2,1:T(8,128)}, u32[]{:S(2)}) copy-start(f32[512,32,40]{0,2,1:T(8,128)} %copy-done.18) | copy-start | bytes 7864324
  278.8 37.7 %copy-start.21 = (f32[512,32,40]{0,2,1:T(8,128)S(1)}, f32[512,32,40]{0,2,1:T(8,128)}, u32[]{:S(2)}) copy-start(f32[512,32,40]{0,2,1:T(8,128)} %copy-done.20) | copy-start | bytes 7864324
  324.7 7.0 %copy-start.8 = (bf16[512,1024]{1,0:T(8,128)(2,1)S(1)}, bf16[512,1024]{1,0:T(8,128)(2,1)}, u32[]{:S(2)}) copy-start(bf16[512,1024]{1,0:T(8,128)(2,1)} %param.21) | copy-start | bytes 3145732
  324.7 42.5 %all-to-all-start.6 = ((bf16[128,1,40,256]{3,2,1,0:T(8,128)(2,1)}), bf16[128,1,40,256]{3,2,1,0:T(8,128)(2,1)}, u32[]{:S(2)}, u32[]{:S(2)}) async-start(bf16[128,1,40,256]{3,2,1,0:T(8,128)(2,1)} %bitcast.281), calls=%async_computation.6 | async-start | bytes 5242880 | tf_op jit(solution)/shard_map/all_to_all | solution.py:64
  331.6 3.2 copy-start.71
  331.6 4.5 copy-start.62
  331.6 180.0 %reduce-scatter.5.cloned.1.call-start = ((), (), s32[]{:S(2)}) async-start(), calls=%async_computation.15 | async-start | bytes 1310720 | tf_op jit(solution)/shard_map/reduce_scatter | solution.py:587
  385.2 9.5 %copy-start.29 = (bf16[32,1,40,512]{3,2,0,1:T(8,128)(2,1)S(1)}, bf16[32,1,40,512]{3,2,0,1:T(8,128)(2,1)}, u32[]{:S(2)}) copy-start(bf16[32,1,40,512]{3,2,0,1:T(8,128)(2,1)} %copy-done.28) | copy-start | bytes 3932164
  390.4 8.6 %collective-permute-start.3 = (bf16[512,256]{1,0:T(8,128)(2,1)S(1)}, bf16[512,256]{1,0:T(8,128)(2,1)S(1)}, u32[]{:S(2)}, u32[]{:S(2)}) collective-permute-start(bf16[512,256]{1,0:T(8,128)(2,1)S(1)} %bitcast_reduce_fusion), channel_id=1, source_target_pairs={{0,1},{1,0},{2,3},{3,2},{4,5},{5,4},{6,7},{7,6},{8,9},{9,8},{10,11... | collective-permute-start | bytes 786440 | tf_op jit(solution)/shard_map/ppermute | solution.py:104
  391.4 9.4 %collective-permute-start.4 = (bf16[512,256]{1,0:T(8,128)(2,1)S(1)}, bf16[512,256]{1,0:T(8,128)(2,1)S(1)}, u32[]{:S(2)}, u32[]{:S(2)}) collective-permute-start(bf16[512,256]{1,0:T(8,128)(2,1)S(1)} %bitcast_reduce_fusion), channel_id=1, source_target_pairs={{0,2},{1,3},{2,0},{3,1},{4,6},{5,7},{6,4},{7,5},{8,10},{9,11},{10,... | collective-permute-start | bytes 786440 | tf_op jit(solution)/shard_map/ppermute | solution.py:104
  392.8 13.8 %collective-permute-start.5 = (bf16[512,256]{1,0:T(8,128)(2,1)S(1)}, bf16[512,256]{1,0:T(8,128)(2,1)S(1)}, u32[]{:S(2)}, u32[]{:S(2)}) collective-permute-start(bf16[512,256]{1,0:T(8,128)(2,1)S(1)} %bitcast_reduce_fusion), channel_id=1, source_target_pairs={{0,3},{1,2},{2,1},{3,0},{4,7},{5,6},{6,5},{7,4},{8,11},{9,10},{10,... | collective-permute-start | bytes 786440 | tf_op jit(solution)/shard_map/ppermute | solution.py:104
  406.6 4.1 copy-start.67
  428.3 22.0 %all-to-all-start.7 = ((bf16[32,48,256]{2,1,0:T(8,128)(2,1)}), bf16[32,48,256]{2,1,0:T(8,128)(2,1)S(1)}, u32[]{:S(2)}, u32[]{:S(2)}) async-start(bf16[32,48,256]{2,1,0:T(8,128)(2,1)} %bitcast.87), calls=%async_computation.7 | async-start | bytes 1572864 | tf_op jit(solution)/shard_map/all_to_all | solution.py:648
  435.2 114.1 %reduce-scatter.7.cloned.1.call-start = ((), (), s32[]{:S(2)}) async-start(), calls=%async_computation.16 | async-start | bytes 2621440
  435.3 3.8 copy-start.34
  452.0 12.4 %copy-start.60 = (bf16[1024]{0:T(1024)(128)(2,1)S(1)}, bf16[1024]{0:T(1024)(128)(2,1)}, u32[]{:S(2)}) copy-start(bf16[1024]{0:T(1024)(128)(2,1)} %get-tuple-element.27) | copy-start | bytes 6148
  454.3 10.6 %copy-start.33 = (bf16[1024,32]{1,0:T(8,128)(2,1)S(1)}, bf16[1024,32]{1,0:T(8,128)(2,1)}, u32[]{:S(2)}) copy-start(bf16[1024,32]{1,0:T(8,128)(2,1)} %copy.152) | copy-start | bytes 196612
  454.3 16.2 %all-to-all-start.8 = ((bf16[32,16,256]{2,1,0:T(8,128)(2,1)}), bf16[32,16,256]{2,1,0:T(8,128)(2,1)S(1)}, u32[]{:S(2)}, u32[]{:S(2)}) async-start(bf16[32,16,256]{2,1,0:T(8,128)(2,1)} %select_reduce_fusion), calls=%async_computation.8 | async-start | bytes 524288 | tf_op jit(solution)/shard_map/all_to_all | solution.py:661
  470.5 26.2 %all-to-all-start.11 = ((bf16[32,32,289]{2,1,0:T(8,128)(2,1)}), bf16[32,32,289]{2,1,0:T(8,128)(2,1)S(1)}, u32[]{:S(2)}, u32[]{:S(2)}) async-start(bf16[32,32,289]{2,1,0:T(8,128)(2,1)} %pad_maximum_fusion.8), calls=%async_computation.11 | async-start | bytes 1572864 | tf_op jit(solution)/shard_map/all_to_all | solution.py:115
  477.2 28.1 %copy-start.26 = (f32[512,8]{1,0:T(8,128)S(1)}, f32[512,8]{1,0:T(8,128)}, u32[]{:S(2)}) copy-start(f32[512,8]{1,0:T(8,128)} %copy-done.25) | copy-start | bytes 49156
  477.2 28.0 %copy-start.51 = (pred[4096]{0:T(1024)(128)(4,1)S(1)}, pred[4096]{0:T(1024)(128)(4,1)}, u32[]{:S(2)}) copy-start(pred[4096]{0:T(1024)(128)(4,1)} %copy-done.50) | copy-start | bytes 12292
  497.6 22.7 %all-to-all-start.9 = ((bf16[4,512,256]{2,1,0:T(8,128)(2,1)}), bf16[4,512,256]{2,1,0:T(8,128)(2,1)S(1)}, u32[]{:S(2)}, u32[]{:S(2)}) async-start(bf16[4,512,256]{2,1,0:T(8,128)(2,1)} %bitcast.274), calls=%async_computation.9 | async-start | bytes 2097152 | tf_op jit(solution)/shard_map/all_to_all | solution.py:115
  505.3 8.2 %copy-start.9 = (bf16[512,1024]{1,0:T(8,128)(2,1)S(1)}, bf16[512,1024]{1,0:T(8,128)(2,1)}, u32[]{:S(2)}) copy-start(bf16[512,1024]{1,0:T(8,128)(2,1)} %param.21) | copy-start | bytes 3145732
  505.3 8.2 %copy-start.56 = (f32[512]{0:T(512)S(1)}, f32[512]{0:T(512)}, u32[]{:S(2)}) copy-start(f32[512]{0:T(512)} %copy-done.54) | copy-start | bytes 6148
  505.3 8.1 %copy-start.70 = (f32[1024]{0:T(1024)S(1)}, f32[1024]{0:T(1024)}, u32[]{:S(2)}) copy-start(f32[1024]{0:T(1024)} %param.25) | copy-start | bytes 12292
  511.5 3.4 copy-start.17
  520.6 7.4 %collective-permute-start.9 = (bf16[512,256]{1,0:T(8,128)(2,1)S(1)}, bf16[512,256]{1,0:T(8,128)(2,1)S(1)}, u32[]{:S(2)}, u32[]{:S(2)}) collective-permute-start(bf16[512,256]{1,0:T(8,128)(2,1)S(1)} %reduce_sum.276), channel_id=1, source_target_pairs={{0,1},{1,0},{2,3},{3,2},{4,5},{5,4},{6,7},{7,6},{8,9},{9,8},{10,11... | collective-permute-start | bytes 786440 | tf_op jit(solution)/shard_map/ppermute | solution.py:104
  521.6 9.4 %collective-permute-start.10 = (bf16[512,256]{1,0:T(8,128)(2,1)S(1)}, bf16[512,256]{1,0:T(8,128)(2,1)S(1)}, u32[]{:S(2)}, u32[]{:S(2)}) collective-permute-start(bf16[512,256]{1,0:T(8,128)(2,1)S(1)} %reduce_sum.276), channel_id=1, source_target_pairs={{0,2},{1,3},{2,0},{3,1},{4,6},{5,7},{6,4},{7,5},{8,10},{9,11},{10,... | collective-permute-start | bytes 786440 | tf_op jit(solution)/shard_map/ppermute | solution.py:104
  521.7 15.1 %collective-permute-start.11 = (bf16[512,256]{1,0:T(8,128)(2,1)S(1)}, bf16[512,256]{1,0:T(8,128)(2,1)S(1)}, u32[]{:S(2)}, u32[]{:S(2)}) collective-permute-start(bf16[512,256]{1,0:T(8,128)(2,1)S(1)} %reduce_sum.276), channel_id=1, source_target_pairs={{0,3},{1,2},{2,1},{3,0},{4,7},{5,6},{6,5},{7,4},{8,11},{9,10},{10,... | collective-permute-start | bytes 786440 | tf_op jit(solution)/shard_map/ppermute | solution.py:104
  544.0 25.9 %all-to-all-start.10 = ((bf16[32,32,513]{2,1,0:T(8,128)(2,1)}), bf16[32,32,513]{2,1,0:T(8,128)(2,1)S(1)}, u32[]{:S(2)}, u32[]{:S(2)}) async-start(bf16[32,32,513]{2,1,0:T(8,128)(2,1)} %pad_maximum_fusion.3), calls=%async_computation.10 | async-start | bytes 2621440 | tf_op jit(solution)/shard_map/all_to_all | solution.py:115
  552.3 3.4 copy-start.65
  (34 other events, 58.6 us)
Sparse Core Ops, SparseCore 0:
  31.5 43.2 all-gather.1
  343.3 33.3 reduce-scatter.4
  450.5 47.6 reduce-scatter.6
